TPU v7x, 32 devices: a whole 2x2x4 slice. The times are simulated.
32 devices in a mesh: gx: 2 (over y), gy: 4 (over z), gz: 4 (over x, core).
Axes of the slice: x: 2, y: 2, z: 4, core: 2. Of those that a mesh axis runs over, the one named last changes fastest.
Arguments:
- features: bfloat16 [16, 4, 4, 64, 128], P('gx', 'gy', 'gz'), may hold values from -6 to 6
- positions: bfloat16 [16, 4, 4, 3, 128], P('gx', 'gy', 'gz'), may hold values from 0 to 1
- counts: int32 [16, 4, 4], P('gx', 'gy', 'gz'), may hold values from 1 to 128, as said below
- old_cuts: int32 [3], replicated, may hold values from 0 to 8, as said below
- new_cuts: int32 [3], replicated, may hold values from 0 to 8, as said below
- radial_rates: float32 [2, 2], replicated, may hold values from 0.3 to 3
- conv_weight: bfloat16 [2, 64, 2, 64], replicated, may hold values from -0.5 to 0.5
- up_weight: bfloat16 [2, 256, 64], replicated, may hold values from -0.75 to 0.75
- up_bias: float32 [2, 256], replicated, may hold values from -3 to 3
- down_weight: bfloat16 [2, 64, 256], replicated, may hold values from -0.375 to 0.375
- down_bias: float32 [2, 64], replicated, may hold values from -2 to 2
Outputs:
- moved: bfloat16 [16, 4, 4, 64, 128], P('gx', 'gy', 'gz')
Inputs may be any that keep to these rules, and one draw needn't show every extreme that they name: `counts`: some bin of the first x layer holds exactly 128 particles. `old_cuts`: rising from 0 to 8; index k of gx holds the x layers from old_cuts[k] to old_cuts[k+1] - 1, from 2 to 8 of them; with three or more indices along gx one holds exactly 8. `new_cuts`: same form as old_cuts, and each cut differs from the one of old_cuts by -1, 0 or 1.
All inputs are finite; a program needn't handle non-finite values.
Results may differ from a plain program's by a relative error of at most 0.0058.
Values may be sent and summed in bfloat16 or wider, within the bound.
No kernel may reach another device: no remote copies, remote signals or barrier semaphores. Data moves between devices by JAX's collectives and lax.ppermute only.
A program may use at most 128 MiB of HBM per device.

v0:
```python
import math

import jax
import jax.numpy as jnp
from jax import lax
from jax.experimental import pallas as pl
from jax.experimental.pallas import tpu as pltpu
from jax.sharding import PartitionSpec as P

EPSILON = 1e-05
FAR = float(2**20)
LOG2E = math.log2(math.e)
HEAD = 8
TERMS = 32
VMEM_LIMIT = 32 * 2**20

MID_START, MID_STOP, LOW, HIGH, MID_AT, OUT_START, OUT_STOP, CUT, COLUMN = range(9)
STEP_Y, STEP_Z, FAR_Y, FAR_Z = 4, 5, 6, 7


def whole():
    return pl.BlockSpec(memory_space=pltpu.VMEM)


def scalars():
    return pl.BlockSpec(memory_space=pltpu.SMEM)


def outside(array):
    return pltpu.with_memory_space_constraint(array, pltpu.HBM)


def params():
    return pltpu.CompilerParams(vmem_limit_bytes=VMEM_LIMIT)


def shift(block, axis, by):
    count = lax.axis_size(axis)
    return lax.ppermute(block, axis, [(i, (i + by) % count) for i in range(count)])


def partner(block, axis):
    count = lax.axis_size(axis)
    return lax.ppermute(block, axis, [(i, i ^ 1) for i in range(count)])


def whole_swap(block, other):
    axes = ("gx", "gy", "gz")
    sizes = [lax.axis_size(axis) for axis in axes]
    pairs = []
    for gx in range(sizes[0]):
        for gy in range(sizes[1]):
            for gz in range(sizes[2]):
                px, py, pz = other(gx, gy, gz, sizes)
                here = (gx * sizes[1] + gy) * sizes[2] + gz
                pairs.append((here, (px * sizes[1] + py) * sizes[2] + pz))
    return lax.ppermute(block, axes, pairs)


def beside(index):
    return ((index + 1) ^ 1) - 1


def other_y(gx, gy, gz, sizes):
    if 0 < gy < sizes[1] - 1:
        return gx, beside(gy), gz
    return gx, gy, gz ^ 1


def other_z(gx, gy, gz, sizes):
    if 0 < gz < sizes[2] - 1:
        return gx, gy, beside(gz)
    return gx ^ 1, gy, gz


def split3(value):
    first = value.astype(jnp.bfloat16).astype(jnp.float32)
    rest = value - first
    second = rest.astype(jnp.bfloat16).astype(jnp.float32)
    return first, second, rest - second


def pack(features, positions, counts, old_cuts, new_cuts, rates, rows):
    slot_rows, _, _, width, slots = features.shape
    peers = lax.axis_size("gx")
    last_y = lax.axis_size("gy") - 1
    last_z = lax.axis_size("gz") - 1
    total = peers * slot_rows // 2

    def body(
        feat_ref,
        pos_in,
        count_in,
        old_in,
        new_in,
        rate_in,
        out_ref,
        int_ref,
        flt_ref,
        pos_ref,
        count_ref,
        old_ref,
        new_ref,
        rate_ref,
        sems,
    ):
        copies = [
            pltpu.make_async_copy(source, target, sems.at[k])
            for k, (source, target) in enumerate(
                (
                    (old_in, old_ref),
                    (new_in, new_ref),
                    (rate_in, rate_ref),
                    (count_in, count_ref),
                    (pos_in, pos_ref),
                    (feat_ref.at[0:rows, 0, 0], out_ref.at[:, 0:width, :]),
                )
            )
        ]
        for copy in copies:
            copy.start()
        for copy in copies[:5]:
            copy.wait()
        column, row_y, row_z = (lax.axis_index(axis) for axis in ("gx", "gy", "gz"))
        new_low, new_high = new_ref[column], new_ref[column + 1]
        if peers == 2:
            base, mid_at = 0, column
        else:
            base, mid_at = new_low - 2, 1
        ints = {
            MID_START: jnp.maximum(new_low - 1, 0) - base,
            MID_STOP: jnp.minimum(new_high + 1, total) - base,
            LOW: jnp.int32(0) - base,
            HIGH: jnp.int32(total) - base,
            MID_AT: jnp.int32(mid_at),
            OUT_START: new_low - base,
            OUT_STOP: new_high - base,
            CUT: old_ref[1],
            COLUMN: column,
        }
        flts = {
            STEP_Y: jnp.where(row_y % 2 == 1, -1.0, 1.0),
            STEP_Z: jnp.where(row_z % 2 == 1, -1.0, 1.0),
            FAR_Y: jnp.where(jnp.logical_or(row_y == 0, row_y == last_y), FAR, 0.0),
            FAR_Z: jnp.where(jnp.logical_or(row_z == 0, row_z == last_z), FAR, 0.0),
        }
        for k in range(2):
            for m in range(2):
                flts[2 * k + m] = rate_ref[k, m]
        lane = lax.broadcasted_iota(jnp.int32, (1, slots), 1)
        line = jnp.zeros((1, slots), jnp.int32)
        for k, value in ints.items():
            line = jnp.where(lane == k, value, line)
        int_ref[...] = line
        line = jnp.zeros((1, slots), jnp.float32)
        for k, value in flts.items():
            line = jnp.where(lane == k, value, line)
        below = jnp.ones((1, slots), jnp.float32)
        for k in range(2):
            below = jnp.where(lane == 2 * k + 1, rate_ref[k, 0], below)
        share = line / below
        flt_ref[...] = share + (line - share * below) / below
        spare = jnp.zeros((HEAD - 4, slots), jnp.float32)
        for row in range(rows):
            place = [pos_ref[d, row : row + 1, :].astype(jnp.float32) for d in range(3)]
            far = jnp.where(lane < count_ref[row], 0.0, FAR)
            block = jnp.concatenate(place + [far, spare], axis=0).astype(jnp.bfloat16)
            out_ref[row, width : width + HEAD, :] = block
        copies[5].wait()

    anywhere = pl.BlockSpec(memory_space=pltpu.HBM)
    return pl.pallas_call(
        body,
        out_shape=(
            jax.ShapeDtypeStruct((rows, width + HEAD, slots), jnp.bfloat16),
            jax.ShapeDtypeStruct((1, slots), jnp.int32),
            jax.ShapeDtypeStruct((1, slots), jnp.float32),
        ),
        in_specs=[anywhere] * 6,
        out_specs=(whole(), whole(), whole()),
        scratch_shapes=[
            pltpu.VMEM((3, slot_rows, slots), positions.dtype),
            pltpu.SMEM((slot_rows,), counts.dtype),
            pltpu.SMEM(old_cuts.shape, old_cuts.dtype),
            pltpu.SMEM(new_cuts.shape, new_cuts.dtype),
            pltpu.SMEM(rates.shape, rates.dtype),
            pltpu.SemaphoreType.DMA((6,)),
        ],
        compiler_params=params(),
    )(
        outside(features),
        outside(jnp.transpose(positions[:, 0, 0], (1, 0, 2))),
        outside(counts.reshape(-1)),
        outside(old_cuts),
        outside(new_cuts),
        outside(rates),
    )


def assemble(ints, mine, other, rows):
    def body(int_ref, mine_ref, other_ref, out_ref):
        cut, column = int_ref[0, CUT], int_ref[0, COLUMN]
        for row in range(rows):
            owner = jnp.int32(row) >= cut
            place = jnp.where(owner, row - cut, row)
            place = jnp.clip(place, 0, mine_ref.shape[0] - 1)
            is_mine = owner.astype(jnp.int32) == column
            out_ref[row] = jnp.where(is_mine, mine_ref[place], other_ref[place])

    return pl.pallas_call(
        body,
        out_shape=jax.ShapeDtypeStruct((rows,) + mine.shape[1:], mine.dtype),
        in_specs=[scalars(), whole(), whole()],
        out_specs=whole(),
        compiler_params=params(),
    )(ints, mine, other)


def stacked(blocks):
    def body(*refs):
        for k in range(len(blocks)):
            for row in range(blocks[0].shape[0]):
                refs[-1][k, row] = refs[k][row]

    return pl.pallas_call(
        body,
        out_shape=jax.ShapeDtypeStruct((len(blocks),) + blocks[0].shape, blocks[0].dtype),
        in_specs=[whole()] * len(blocks),
        out_specs=whole(),
        compiler_params=params(),
    )(*blocks)


def centre_terms(place, along, row8, spread):
    here = place.astype(jnp.float32)
    live = row8 < 3
    at = jnp.where(row8 == 0, here + along, jnp.where(live, here, 0.0))
    norm = jnp.sum(at * at, axis=0, keepdims=True)
    rows = jnp.where(row8 == 3, norm, -2.0 * at)
    stack = jnp.concatenate(split3(rows) + (jnp.zeros_like(rows),), axis=0)
    return jnp.dot(stack.T.astype(jnp.bfloat16), spread, preferred_element_type=jnp.float32)


def near_terms(place, base, along, gone, row8):
    there = place.astype(jnp.float32)
    far = there[3:4, :] + gone
    at = jnp.where(row8 == 0, there + along, jnp.where(row8 < 3, there - base, 0.0))
    norm = jnp.sum(at * at, axis=0, keepdims=True)
    norm = jnp.where(far > 0.0, FAR * FAR, norm)
    return jnp.where(row8 == 3, norm, at)


def gather_bins(rows, scales, near_ref, feats, centre_ref, feat_at):
    sums = []
    scale, ratio = scales
    for row in rows:
        minus = [centre_ref[row, k] for k in range(3)]
        norm = centre_ref[row, 3] * scale
        items = [(c, dx) for c in range(len(feats)) for dx in range(3)]
        total = None
        for k in range(0, len(items), 2):
            weights = [[], []]
            vals = []
            for c, dx in items[k : k + 2]:
                near = near_ref[c, row + dx] * scale
                power = norm + near[3:4, :]
                for d in range(3):
                    power = power + minus[d] * near[d : d + 1, :]
                weights[0].append(jnp.exp2(power).astype(jnp.bfloat16))
                weights[1].append(jnp.exp2(power * ratio).astype(jnp.bfloat16))
                source = jnp.clip(row + dx - 1 - feat_at, 0, feats[c].shape[0] - 1)
                vals.append(feats[c][source, :, :])
            if len(vals) == 1:
                feat = vals[0]
                sides = [group[0] for group in weights]
            else:
                feat = jnp.concatenate(vals, axis=1)
                sides = [jnp.concatenate(group, axis=1) for group in weights]
            part = lax.dot_general(
                feat,
                jnp.concatenate(sides, axis=0),
                (((1,), (1,)), ((), ())),
                preferred_element_type=jnp.float32,
            )
            total = part if total is None else total + part
        sums.append(total)
    return sums


def views(spec, arrays, start, size):
    found = []
    for index, sub, *_ in spec:
        ref = arrays[index] if sub is None else arrays[index].at[sub]
        found.append(ref.at[:, start : start + size, :])
    return found


def gather_call(stage, level, ints, flts, spec, frame, feats, right, near, before, extra, out_rows):
    frame_rows, tall, slots = frame.shape
    features = tall - HEAD
    centre = frame_rows // 2
    make_right = right is None
    make_near = near is None
    inputs = [frame] + list(feats)
    if not make_right:
        inputs.append(right)
    if not make_near:
        inputs.append(near)
    if before is not None:
        inputs.append(before)
    inputs += list(extra)
    outs = []
    wide = 2 * slots
    if stage < 2:
        outs.append(jax.ShapeDtypeStruct((out_rows, features, wide), jnp.float32))
    else:
        outs.append(jax.ShapeDtypeStruct((out_rows, features, slots), jnp.bfloat16))
    if make_right:
        outs.append(jax.ShapeDtypeStruct((frame_rows, 4, slots, slots), jnp.float32))
    if make_near:
        outs.append(
            jax.ShapeDtypeStruct((len(spec), frame_rows + 2, HEAD, slots), jnp.float32)
        )
    if stage == 0:
        hid = extra[0].shape[2]
        outs.append(jax.ShapeDtypeStruct((features, 2 * features), jnp.bfloat16))
        outs.append(jax.ShapeDtypeStruct((hid, features), jnp.bfloat16))
        outs.append(jax.ShapeDtypeStruct((hid, wide), jnp.float32))
        outs.append(jax.ShapeDtypeStruct((features, wide), jnp.float32))

    def body(*refs):
        refs = list(refs)
        ints, flts = refs.pop(0).at[0], refs.pop(0).at[0]
        home = refs.pop(0)
        vals = [refs.pop(0) for _ in feats]
        right_ref = None if make_right else refs.pop(0)
        near_ref = None if make_near else refs.pop(0)
        prior = None if before is None else refs.pop(0)
        extras = [refs.pop(0) for _ in extra]
        out_ref = refs.pop(0)
        right_ref = refs.pop(0) if make_right else right_ref
        near_ref = refs.pop(0) if make_near else near_ref
        start, stop = (
            (ints[MID_START], ints[MID_STOP]) if level == 0 else (ints[OUT_START], ints[OUT_STOP])
        )
        out_at = ints[MID_AT] if level == 0 else ints[OUT_START]
        feat_at = jnp.int32(0) if level == 0 else ints[MID_AT]
        if stage == 0:
            held = refs[4:8]
            copies = [
                pltpu.make_async_copy(source, target, refs[8].at[k])
                for k, (source, target) in enumerate(zip(extras, held))
            ]
            for copy in copies:
                copy.start()
        row8 = lax.broadcasted_iota(jnp.int32, (HEAD, slots), 0)
        scales = [flts[2 * level] * -LOG2E, flts[2 * level + 1]]

        if make_right:
            kind = lax.broadcasted_iota(jnp.int32, (TERMS, 4 * slots), 0)
            lane = lax.broadcasted_iota(jnp.int32, (TERMS, 4 * slots), 1)
            spread = jnp.where(
                jnp.logical_and(kind % HEAD == lane // slots, kind < 3 * HEAD), 1.0, 0.0
            ).astype(jnp.bfloat16)
            for row in range(frame_rows):
                place = home[row, features:tall, :]
                terms = centre_terms(place, float(centre - row), row8, spread)
                for k in range(4):
                    right_ref[row, k] = terms[:, k * slots : (k + 1) * slots]
        if make_near:
            edge = jnp.where(row8 == 3, FAR * FAR, 0.0)
            wheres = views(spec, vals, features, HEAD)
            for c, (_, _, dy, dz, flags) in enumerate(spec):
                near_ref[c, 0] = edge
                near_ref[c, frame_rows + 1] = edge
                gone = jnp.float32(0.0)
                for flag in flags:
                    gone = gone + flts[flag]
                base = jnp.where(row8 == 1, float(dy) * flts[STEP_Y], 0.0)
                base = jnp.where(row8 == 2, float(dz) * flts[STEP_Z], base)
                for row in range(frame_rows):
                    inside = jnp.logical_and(row >= ints[LOW], row < ints[HIGH])
                    lost = gone + jnp.where(inside, 0.0, FAR)
                    near_ref[c, row + 1] = near_terms(
                        wheres[c][row, :, :], base, float(centre - row), lost, row8
                    )
        heads = views(spec, vals, 0, features)

        def pair(turn):
            return [start + 2 * turn, start + 2 * turn + 1]

        turns = (stop - start) // 2
        odd = (stop - start) % 2
        if stage < 2:

            def gather(rows):
                sums = gather_bins(rows, scales, near_ref, heads, right_ref, feat_at)
                for row, total in zip(rows, sums):
                    if prior is not None:
                        total = total + prior[row - out_at]
                    out_ref[row - out_at] = total

            def step(turn, carry):
                gather(pair(turn))
                return carry

            lax.fori_loop(0, turns, step, 0)

            @pl.when(odd == 1)
            def _():
                gather([stop - 1])

            if stage == 0:
                wconv_ref, wup_ref, wupb_ref, wdownb_ref = refs[:4]
                up_ref, upb_ref, downb_ref, conv_in = held
                for copy in copies:
                    copy.wait()
                wconv_ref[...] = jnp.concatenate(
                    [conv_in[level, :, m, :] for m in range(2)], axis=1
                )
                wup_ref[...] = up_ref[level].astype(jnp.float32).T.astype(jnp.bfloat16)
                lift = jnp.broadcast_to(upb_ref[level : level + 1, :], (slots, upb_ref.shape[1])).T
                wupb_ref[...] = jnp.concatenate([lift, lift], axis=1)
                low = jnp.broadcast_to(downb_ref[level : level + 1, :], (slots, features))
                low = jnp.concatenate([low, low], axis=1).T[0:features, :]
                wdownb_ref[...] = jnp.concatenate([low, low], axis=1)

            return

        centre_ref, down_ref, conv_ref, wup_ref, wupb_ref, wdownb_ref = extras
        gath_ref = refs[0]

        def finish(rows, slot):
            size = len(rows) * slots
            packed = gath_ref[slot, :, 0:size]
            mixed = jnp.dot(conv_ref[...], packed, preferred_element_type=jnp.float32)
            centred = mixed - jnp.mean(mixed, axis=0, keepdims=True)
            spread = jnp.mean(centred * centred, axis=0, keepdims=True)
            normed = (centred * lax.rsqrt(spread + EPSILON)).astype(jnp.bfloat16)
            hidden = jnp.dot(wup_ref[...], normed, preferred_element_type=jnp.float32)
            half = 0.5 * (hidden + wupb_ref[:, 0:size])
            hidden = (half + half * jnp.tanh(half)).astype(jnp.bfloat16)
            update = jnp.dot(down_ref[level], hidden, preferred_element_type=jnp.float32)
            update = update + wdownb_ref[:, 0:size]
            for k, row in enumerate(rows):
                source = jnp.clip(row - feat_at, 0, centre_ref.shape[0] - 1)
                kept = centre_ref[source, 0:features, :].astype(jnp.float32)
                far = home[row, features:tall, :].astype(jnp.float32)[3:4, :]
                result = kept + update[:, k * slots : (k + 1) * slots]
                out_ref[row - out_at] = jnp.where(far == 0.0, result, 0.0).astype(jnp.bfloat16)

        for place in range(out_rows):
            out_ref[place] = jnp.zeros((features, slots), jnp.bfloat16)

        def gather(rows, slot, last):
            sums = gather_bins(rows, scales, near_ref, heads, right_ref, feat_at)
            finish(pair(last), 1 - slot)
            both = []
            for row, total in zip(rows, sums):
                total = total + prior[row - out_at]
                both.append(jnp.concatenate([total[:, :slots], total[:, slots:]], axis=0))
            both = both[0] if len(both) == 1 else jnp.concatenate(both, axis=1)
            gath_ref[slot, :, 0 : len(rows) * slots] = both.astype(jnp.bfloat16)

        def step(turn, carry):
            gather(pair(turn), turn % 2, jnp.maximum(turn - 1, 0))
            return carry

        lax.fori_loop(0, turns, step, 0)

        @pl.when(odd == 1)
        def _():
            gather([stop - 1], turns % 2, turns - 1)
            finish([stop - 1], turns % 2)

        @pl.when(odd == 0)
        def _():
            finish(pair(turns - 1), (turns + 1) % 2)

    pairs = out_rows * 3 * len(spec)
    specs = [whole()] * len(inputs)
    scratch = []
    if stage == 0:
        scratch = [pltpu.VMEM(array.shape, array.dtype) for array in extra]
        scratch.append(pltpu.SemaphoreType.DMA((len(extra),)))
        specs[len(inputs) - len(extra) :] = [pl.BlockSpec(memory_space=pltpu.HBM)] * len(extra)
    if stage == 2:
        scratch = [pltpu.VMEM((2, 2 * features, wide), jnp.bfloat16)]
    return pl.pallas_call(
        body,
        out_shape=tuple(outs),
        in_specs=[scalars(), scalars()] + specs,
        out_specs=tuple(whole() for _ in outs),
        scratch_shapes=scratch,
        cost_estimate=pl.CostEstimate(
            flops=pairs * 2 * slots * slots * (2 * features + HEAD),
            transcendentals=pairs * 2 * slots * slots,
            bytes_accessed=pairs * 4 * slots * slots,
        ),
        compiler_params=params(),
    )(ints, flts, *inputs)


def local(
    features,
    positions,
    counts,
    old_cuts,
    new_cuts,
    radial_rates,
    conv_weight,
    up_weight,
    up_bias,
    down_weight,
    down_bias,
):
    peers = lax.axis_size("gx")
    slot_rows = features.shape[0]
    total = peers * slot_rows // 2
    most = min(slot_rows, total - 2 * (peers - 1))
    packed, ints, flts = pack(
        features, positions, counts, old_cuts, new_cuts, radial_rates, most
    )

    if peers == 2:
        other = lax.ppermute(packed, "gx", [(0, 1), (1, 0)])
        frame = assemble(ints, packed, other, total)
        mid_rows = total - 1
    else:
        column = lax.axis_index("gx")
        old_low = old_cuts[column]
        old_high = old_cuts[column + 1]
        held = old_high - old_low
        frame_rows = slot_rows + 4
        base = new_cuts[column] - 2
        pieces = [packed]
        starts = [old_low]
        for by, rows in ((1, 3), (2, 1)):
            tail_at = jnp.maximum(held - rows, 0)
            tail = lax.dynamic_slice_in_dim(packed, tail_at, rows, 0)
            pieces.append(shift(tail, "gx", by))
            back = jnp.maximum(column - by, 0)
            starts.append(jnp.maximum(old_cuts[back], old_cuts[back + 1] - rows))
            pieces.append(shift(packed[:rows], "gx", -by))
            starts.append(old_cuts[jnp.minimum(column + by, peers - 1)])
        layer = base + jnp.arange(frame_rows, dtype=jnp.int32)
        before = old_cuts[jnp.maximum(column - 1, 0)]
        after = old_cuts[jnp.minimum(column + 1, peers - 1) + 1]
        at = []
        first = 0
        for piece, begin in zip(pieces, starts):
            at.append(first + layer - begin)
            first += piece.shape[0]
        choice = jnp.where(
            layer >= old_high,
            jnp.where(layer >= after, at[4], at[2]),
            jnp.where(layer >= old_low, at[0], jnp.where(layer >= before, at[1], at[3])),
        )
        frame = jnp.take(jnp.concatenate(pieces, axis=0), jnp.clip(choice, 0, first - 1), axis=0)
        mid_rows = slot_rows + 2

    own = [(0, None, 0, 0, ())]
    sides = [
        (0, None, -1, 0, (FAR_Y,)),
        (1, None, 1, 0, ()),
        (2, 0, 0, 1, ()),
        (2, 1, -1, 1, (FAR_Y,)),
        (2, 2, 1, 1, ()),
    ]
    cross = [
        (0, 0, 0, -1, (FAR_Z,)),
        (0, 1, -1, -1, (FAR_Y, FAR_Z)),
        (0, 2, 1, -1, (FAR_Z,)),
    ]
    up_turned = jnp.transpose(up_weight, (0, 2, 1))

    def layer_of(level, block, known, out_rows):
        up = whole_swap(block, other_y)
        down = partner(block, "gy")
        right, near0, near1, near2 = known
        made = gather_call(
            0,
            level,
            ints,
            flts,
            own,
            frame,
            [block],
            right,
            near0,
            None,
            [outside(array) for array in (up_turned, up_bias, down_bias, conv_weight)],
            out_rows,
        )
        acc, made = made[0], list(made[1:])
        if level == 0:
            right, near0 = made[:2]
        ready = made[-4:]
        acc, up, down = lax.optimization_barrier((acc, up, down))
        trio = stacked([block, up, down])
        close = partner(trio, "gz")
        far = whole_swap(trio, other_z)
        made = gather_call(
            1, level, ints, flts, sides, frame, [up, down, close], right, near1, acc, [], out_rows
        )
        acc = made[0]
        if level == 0:
            near1 = made[1]
        made = gather_call(
            2,
            level,
            ints,
            flts,
            cross,
            frame,
            [far],
            right,
            near2,
            acc,
            [block, down_weight] + ready,
            out_rows,
        )
        if level == 0:
            near2 = made[1]
        return made[0], (right, near0, near1, near2)

    mid, known = layer_of(0, frame, (None,) * 4, mid_rows)
    moved, _ = layer_of(1, mid, known, slot_rows)
    return moved[:, None, None]


def solution(mesh):
    placed = (P("gx", "gy", "gz", None, None),) * 2 + (P("gx", "gy", "gz"),) + (P(),) * 8
    return jax.shard_map(
        local,
        mesh=mesh,
        in_specs=placed,
        out_specs=P("gx", "gy", "gz", None, None),
        check_vma=False,
    )
```

profile of v0, /device:TPU:1, one launch (start us, length us, event | category | flops | bytes accessed | tf_op | source)
XLA Modules:
  0.0 43.3 jit_solution(9719653446512166108)
XLA Ops:
  0.0 1.0 %shard_map.109 = (bf16[6,72,128]{2,1,0:T(8,128)(2,1)S(1)}, s32[1,128]{1,0:T(1,128)S(1)}, f32[1,128]{1,0:T(1,128)S(1)}) custom-call(bf16[8,1,1,64,128]{4,3,2,1,0:T(8,128)(2,1)} %feat_ref.1, bf16[3,8,128]{2,1,0:T(8,128)(2,1)} %bitcast.10, s32[8]{0:T(128)} %bitcast.11, s32[3]{0:T(128)} %old_in.1, s32[3]{0:T(128)} %new_in.1, f32[2,2]{1,0:T(2,128)} %rate_in.1), custom_call_target="tpu_custom_call" | custom-call | tf_op jit(solution)/shard_map/pallas_call | solution.py:172
  1.0 2.1 %collective-permute-start = (bf16[6,72,128]{2,1,0:T(8,128)(2,1)S(1)}, bf16[6,72,128]{2,1,0:T(8,128)(2,1)S(1)}, u32[]{:S(2)}, u32[]{:S(2)}) collective-permute-start(bf16[6,72,128]{2,1,0:T(8,128)(2,1)S(1)} %get-tuple-element.32.mine_ref), channel_id=1, source_target_pairs={{0,16},{16,0},{1,17},{17,1},{2,18},{18,2},{3,19},{19,3},{4,20},{20... | collective-permute-start | bytes 331784 | tf_op jit(solution)/shard_map/ppermute | solution.py:526
  3.1 2.8 %collective-permute-done.other_ref = bf16[6,72,128]{2,1,0:T(8,128)(2,1)S(1)} collective-permute-done((bf16[6,72,128]{2,1,0:T(8,128)(2,1)S(1)}, bf16[6,72,128]{2,1,0:T(8,128)(2,1)S(1)}, u32[]{:S(2)}, u32[]{:S(2)}) %collective-permute-start) | collective-permute-done | bytes 110624 | tf_op jit(solution)/shard_map/ppermute | solution.py:526
  5.9 0.6 %shard_map.110.refs_2_.refs_3_.refs_0_.refs_6_ = bf16[8,72,128]{2,1,0:T(8,128)(2,1)S(1)} custom-call(s32[1,128]{1,0:T(1,128)S(1)} %get-tuple-element.30.int_ref.refs_0_, bf16[6,72,128]{2,1,0:T(8,128)(2,1)S(1)} %get-tuple-element.32.mine_ref, bf16[6,72,128]{2,1,0:T(8,128)(2,1)S(1)} %collective-permute-done.other_ref), custom_call_target="tpu_custom_call" | custom-call | tf_op jit(solution)/shard_map/pallas_call | solution.py:210
  6.5 1.3 %collective-permute-start.2 = (bf16[8,72,128]{2,1,0:T(8,128)(2,1)S(1)}, bf16[8,72,128]{2,1,0:T(8,128)(2,1)S(1)}, u32[]{:S(2)}, u32[]{:S(2)}) collective-permute-start(bf16[8,72,128]{2,1,0:T(8,128)(2,1)S(1)} %shard_map.110.refs_2_.refs_3_.refs_0_.refs_6_), channel_id=1, source_target_pairs={{0,4},{4,0},{8,12},{12,8},{1,5},{5,1},{9,13},{13,9},{2,6},{6,2},{1... | collective-permute-start | bytes 442376 | tf_op jit(solution)/shard_map/ppermute | solution.py:44
  7.8 1.8 %collective-permute-start.1 = (bf16[8,72,128]{2,1,0:T(8,128)(2,1)S(1)}, bf16[8,72,128]{2,1,0:T(8,128)(2,1)S(1)}, u32[]{:S(2)}, u32[]{:S(2)}) collective-permute-start(bf16[8,72,128]{2,1,0:T(8,128)(2,1)S(1)} %shard_map.110.refs_2_.refs_3_.refs_0_.refs_6_), channel_id=1, source_target_pairs={{0,1},{1,0},{2,3},{3,2},{4,8},{5,9},{6,10},{7,11},{8,4},{9,5},{10,... | collective-permute-start | bytes 442376 | tf_op jit(solution)/shard_map/ppermute | solution.py:57
  9.6 2.3 %shard_map.111 = (f32[7,64,256]{2,1,0:T(8,128)S(1)}, f32[8,4,128,128]{3,2,1,0:T(8,128)S(1)}, f32[1,10,8,128]{3,2,1,0:T(8,128)S(1)}, bf16[64,128]{1,0:T(8,128)(2,...) custom-call(s32[1,128]{1,0:T(1,128)S(1)} %get-tuple-element.30.int_ref.refs_0_, ...), custom_call_target="tpu_custom_call" | custom-call | flops 93585408 | bytes 1376256 | tf_op jit(solution)/shard_map/pallas_call | solution.py:489
  11.9 0.0 collective-permute-done.2.refs_2_.refs_4_
  11.9 0.0 collective-permute-done.1.refs_1_.refs_3_
  11.9 1.1 %collective-permute-start.4 = (bf16[3,8,72,128]{3,2,1,0:T(8,128)(2,1)S(1)}, bf16[3,8,72,128]{3,2,1,0:T(8,128)(2,1)S(1)}, u32[]{:S(2)}, u32[]{:S(2)}) collective-permute-start(bf16[3,8,72,128]{3,2,1,0:T(8,128)(2,1)S(1)} %shard_map.112), channel_id=1, source_target_pairs={{0,1},{1,0},{2,3},{3,2},{4,5},{5,4},{6,7},{7,6},{8,9},{9,8},{10,11... | collective-permute-start | bytes 1327112 | tf_op jit(solution)/shard_map/ppermute | solution.py:44
  13.0 1.4 %collective-permute-start.3 = (bf16[3,8,72,128]{3,2,1,0:T(8,128)(2,1)S(1)}, bf16[3,8,72,128]{3,2,1,0:T(8,128)(2,1)S(1)}, u32[]{:S(2)}, u32[]{:S(2)}) collective-permute-start(bf16[3,8,72,128]{3,2,1,0:T(8,128)(2,1)S(1)} %shard_map.112), channel_id=1, source_target_pairs={{0,16},{1,2},{2,1},{3,19},{4,20},{5,6},{6,5},{7,23},{8,24},{9,10},... | collective-permute-start | bytes 1327112 | tf_op jit(solution)/shard_map/ppermute | solution.py:57
  14.4 0.0 collective-permute-done.4.refs_5_
  14.5 0.0 copy-start
  14.5 3.4 %shard_map.113 = (f32[7,64,256]{2,1,0:T(8,128)S(1)}, f32[5,10,8,128]{3,2,1,0:T(8,128)S(1)}) custom-call(s32[1,128]{1,0:T(1,128)S(1)} %get-tuple-element.30.int_ref.refs_0_, f32[1,128]{1,0:T(1,128)S(1)} %get-tuple-element.31.refs_1_, bf16[8,72,128]{2,1,0:T(8,128)(2,1)S(1)} %shard_map.110.refs_2_.refs_3_.refs_0_.refs_6_, ...), custom_call_target="tpu_custom_call" | custom-call | flops 467927040 | bytes 6881280 | tf_op jit(solution)/shard_map/pallas_call | solution.py:489
  17.9 3.1 %collective-permute-done.3.refs_3_ = bf16[3,8,72,128]{3,2,1,0:T(8,128)(2,1)S(1)} collective-permute-done((bf16[3,8,72,128]{3,2,1,0:T(8,128)(2,1)S(1)}, bf16[3,8,72,128]{3,2,1,0:T(8,128)(2,1)S(1)}, u32[]{:S(2)}, u32[]{:S(2)}) %collective-permute-start.3) | collective-permute-done | bytes 442400 | tf_op jit(solution)/shard_map/ppermute | solution.py:57
  21.0 0.0 copy-done
  21.0 4.2 %shard_map.114 = (bf16[7,64,128]{2,1,0:T(8,128)(2,1)S(1)}, f32[3,10,8,128]{3,2,1,0:T(8,128)S(1)}) custom-call(s32[1,128]{1,0:T(1,128)S(1)} %get-tuple-element.30.int_ref.refs_0_, f32[1,128]{1,0:T(1,128)S(1)} %get-tuple-element.31.refs_1_, bf16[8,72,128]{2,1,0:T(8,128)(2,1)S(1)} %shard_map.110.refs_2_.refs_3_.refs_0_.refs_6_, ...), custom_call_target="tpu_custom_call" | custom-call | flops 280756224 | bytes 4128768 | tf_op jit(solution)/shard_map/pallas_call | solution.py:489
  25.2 2.7 %collective-permute-start.6 = (bf16[7,64,128]{2,1,0:T(8,128)(2,1)S(1)}, bf16[7,64,128]{2,1,0:T(8,128)(2,1)S(1)}, u32[]{:S(2)}, u32[]{:S(2)}) collective-permute-start(bf16[7,64,128]{2,1,0:T(8,128)(2,1)S(1)} %get-tuple-element.43.refs_3_.refs_0_.refs_7_), channel_id=1, source_target_pairs={{0,4},{4,0},{8,12},{12,8},{1,5},{5,1},{9,13},{13,9},{2,6},{6,2},{1... | collective-permute-start | bytes 344072 | tf_op jit(solution)/shard_map/ppermute | solution.py:44
  27.9 0.7 %collective-permute-start.5 = (bf16[7,64,128]{2,1,0:T(8,128)(2,1)S(1)}, bf16[7,64,128]{2,1,0:T(8,128)(2,1)S(1)}, u32[]{:S(2)}, u32[]{:S(2)}) collective-permute-start(bf16[7,64,128]{2,1,0:T(8,128)(2,1)S(1)} %get-tuple-element.43.refs_3_.refs_0_.refs_7_), channel_id=1, source_target_pairs={{0,1},{1,0},{2,3},{3,2},{4,8},{5,9},{6,10},{7,11},{8,4},{9,5},{10,... | collective-permute-start | bytes 344072 | tf_op jit(solution)/shard_map/ppermute | solution.py:57
  28.6 1.7 %shard_map.115 = (f32[8,64,256]{2,1,0:T(8,128)S(1)}, bf16[64,128]{1,0:T(8,128)(2,1)S(1)}, bf16[256,64]{1,0:T(8,128)(2,1)S(1)}, f32[256,256]{1,0:T(8,128)S(1)}, f32[64,256]{1,0:T(8,128)S(1)}) custom-call(s32[1,128]{1,0:T(1,128)S(1)} %get-tuple-element.30.int_ref.refs_0_, f32[1,128]{1,0:T(1,128)S(1)} %get-tuple-element.31.refs_1_, ...), custom_call_target="tpu_custom_call" | custom-call | flops 106954752 | bytes 1572864 | tf_op jit(solution)/shard_map/pallas_call | solution.py:489
  30.3 0.8 %collective-permute-done.6.refs_2_.refs_4_ = bf16[7,64,128]{2,1,0:T(8,128)(2,1)S(1)} collective-permute-done((bf16[7,64,128]{2,1,0:T(8,128)(2,1)S(1)}, bf16[7,64,128]{2,1,0:T(8,128)(2,1)S(1)}, u32[]{:S(2)}, u32[]{:S(2)}) %collective-permute-start.6) | collective-permute-done | bytes 114720 | tf_op jit(solution)/shard_map/ppermute | solution.py:44
  31.0 0.0 collective-permute-done.5.refs_1_.refs_3_
  31.1 1.0 %collective-permute-start.8 = (bf16[3,7,64,128]{3,2,1,0:T(8,128)(2,1)S(1)}, bf16[3,7,64,128]{3,2,1,0:T(8,128)(2,1)S(1)}, u32[]{:S(2)}, u32[]{:S(2)}) collective-permute-start(bf16[3,7,64,128]{3,2,1,0:T(8,128)(2,1)S(1)} %shard_map.116), channel_id=1, source_target_pairs={{0,1},{1,0},{2,3},{3,2},{4,5},{5,4},{6,7},{7,6},{8,9},{9,8},{10,11... | collective-permute-start | bytes 1032200 | tf_op jit(solution)/shard_map/ppermute | solution.py:44
  32.1 0.6 %collective-permute-start.7 = (bf16[3,7,64,128]{3,2,1,0:T(8,128)(2,1)S(1)}, bf16[3,7,64,128]{3,2,1,0:T(8,128)(2,1)S(1)}, u32[]{:S(2)}, u32[]{:S(2)}) collective-permute-start(bf16[3,7,64,128]{3,2,1,0:T(8,128)(2,1)S(1)} %shard_map.116), channel_id=1, source_target_pairs={{0,16},{1,2},{2,1},{3,19},{4,20},{5,6},{6,5},{7,23},{8,24},{9,10},... | collective-permute-start | bytes 1032200 | tf_op jit(solution)/shard_map/ppermute | solution.py:57
  32.7 0.7 %collective-permute-done.8.refs_5_ = bf16[3,7,64,128]{3,2,1,0:T(8,128)(2,1)S(1)} collective-permute-done((bf16[3,7,64,128]{3,2,1,0:T(8,128)(2,1)S(1)}, bf16[3,7,64,128]{3,2,1,0:T(8,128)(2,1)S(1)}, u32[]{:S(2)}, u32[]{:S(2)}) %collective-permute-start.8) | collective-permute-done | bytes 344096 | tf_op jit(solution)/shard_map/ppermute | solution.py:44
  33.4 2.9 %shard_map.117.refs_6_ = f32[8,64,256]{2,1,0:T(8,128)S(1)} custom-call(s32[1,128]{1,0:T(1,128)S(1)} %get-tuple-element.30.int_ref.refs_0_, f32[1,128]{1,0:T(1,128)S(1)} %get-tuple-element.31.refs_1_, bf16[8,72,128]{2,1,0:T(8,128)(2,1)S(1)} %shard_map.110.refs_2_.refs_3_.refs_0_.refs_6_, bf16[7,64,128]{2,1,0:T(8,128)(2,1)S(1)} %collective-permute-done.5.refs_1_.refs_3_, ...), custom_call_target="tpu_custom_call" | custom-call | flops 534773760 | bytes 7864320 | tf_op jit(solution)/shard_map/pallas_call | solution.py:489
  36.4 2.7 %collective-permute-done.7.refs_3_ = bf16[3,7,64,128]{3,2,1,0:T(8,128)(2,1)S(1)} collective-permute-done((bf16[3,7,64,128]{3,2,1,0:T(8,128)(2,1)S(1)}, bf16[3,7,64,128]{3,2,1,0:T(8,128)(2,1)S(1)}, u32[]{:S(2)}, u32[]{:S(2)}) %collective-permute-start.7) | collective-permute-done | bytes 344096 | tf_op jit(solution)/shard_map/ppermute | solution.py:57
  39.1 4.2 %shard_map.118 = bf16[8,64,128]{2,1,0:T(8,128)(2,1)} custom-call(s32[1,128]{1,0:T(1,128)S(1)} %get-tuple-element.30.int_ref.refs_0_, f32[1,128]{1,0:T(1,128)S(1)} %get-tuple-element.31.refs_1_, bf16[8,72,128]{2,1,0:T(8,128)(2,1)S(1)} %shard_map.110.refs_2_.refs_3_.refs_0_.refs_6_, bf16[3,7,64,128]{3,2,1,0:T(8,128)(2,1)S(1)} %collective-permute-done.7.refs_3_, ...), custom_call_target="tpu_custom_call" | custom-call | flops 320864256 | bytes 4718592 | tf_op jit(solution)/shard_map/pallas_call | solution.py:489
  (2 shorter events, 0.1 us)
Async XLA Ops:
  1.0 4.9 %collective-permute-start = (bf16[6,72,128]{2,1,0:T(8,128)(2,1)S(1)}, bf16[6,72,128]{2,1,0:T(8,128)(2,1)S(1)}, u32[]{:S(2)}, u32[]{:S(2)}) collective-permute-start(bf16[6,72,128]{2,1,0:T(8,128)(2,1)S(1)} %get-tuple-element.32.mine_ref), channel_id=1, source_target_pairs={{0,16},{16,0},{1,17},{17,1},{2,18},{18,2},{3,19},{19,3},{4,20},{20... | collective-permute-start | bytes 331784 | tf_op jit(solution)/shard_map/ppermute | solution.py:526
  6.5 5.4 %collective-permute-start.2 = (bf16[8,72,128]{2,1,0:T(8,128)(2,1)S(1)}, bf16[8,72,128]{2,1,0:T(8,128)(2,1)S(1)}, u32[]{:S(2)}, u32[]{:S(2)}) collective-permute-start(bf16[8,72,128]{2,1,0:T(8,128)(2,1)S(1)} %shard_map.110.refs_2_.refs_3_.refs_0_.refs_6_), channel_id=1, source_target_pairs={{0,4},{4,0},{8,12},{12,8},{1,5},{5,1},{9,13},{13,9},{2,6},{6,2},{1... | collective-permute-start | bytes 442376 | tf_op jit(solution)/shard_map/ppermute | solution.py:44
  7.8 4.1 %collective-permute-start.1 = (bf16[8,72,128]{2,1,0:T(8,128)(2,1)S(1)}, bf16[8,72,128]{2,1,0:T(8,128)(2,1)S(1)}, u32[]{:S(2)}, u32[]{:S(2)}) collective-permute-start(bf16[8,72,128]{2,1,0:T(8,128)(2,1)S(1)} %shard_map.110.refs_2_.refs_3_.refs_0_.refs_6_), channel_id=1, source_target_pairs={{0,1},{1,0},{2,3},{3,2},{4,8},{5,9},{6,10},{7,11},{8,4},{9,5},{10,... | collective-permute-start | bytes 442376 | tf_op jit(solution)/shard_map/ppermute | solution.py:57
  11.9 2.5 %collective-permute-start.4 = (bf16[3,8,72,128]{3,2,1,0:T(8,128)(2,1)S(1)}, bf16[3,8,72,128]{3,2,1,0:T(8,128)(2,1)S(1)}, u32[]{:S(2)}, u32[]{:S(2)}) collective-permute-start(bf16[3,8,72,128]{3,2,1,0:T(8,128)(2,1)S(1)} %shard_map.112), channel_id=1, source_target_pairs={{0,1},{1,0},{2,3},{3,2},{4,5},{5,4},{6,7},{7,6},{8,9},{9,8},{10,11... | collective-permute-start | bytes 1327112 | tf_op jit(solution)/shard_map/ppermute | solution.py:44
  13.0 8.0 %collective-permute-start.3 = (bf16[3,8,72,128]{3,2,1,0:T(8,128)(2,1)S(1)}, bf16[3,8,72,128]{3,2,1,0:T(8,128)(2,1)S(1)}, u32[]{:S(2)}, u32[]{:S(2)}) collective-permute-start(bf16[3,8,72,128]{3,2,1,0:T(8,128)(2,1)S(1)} %shard_map.112), channel_id=1, source_target_pairs={{0,16},{1,2},{2,1},{3,19},{4,20},{5,6},{6,5},{7,23},{8,24},{9,10},... | collective-permute-start | bytes 1327112 | tf_op jit(solution)/shard_map/ppermute | solution.py:57
  14.5 6.6 %copy-start = (bf16[2,64,256]{2,1,0:T(8,128)(2,1)S(1)}, bf16[2,64,256]{2,1,0:T(8,128)(2,1)}, u32[]{:S(2)}) copy-start(bf16[2,64,256]{2,1,0:T(8,128)(2,1)} %refs_8_.3) | copy-start | bytes 196612
  25.2 5.8 %collective-permute-start.6 = (bf16[7,64,128]{2,1,0:T(8,128)(2,1)S(1)}, bf16[7,64,128]{2,1,0:T(8,128)(2,1)S(1)}, u32[]{:S(2)}, u32[]{:S(2)}) collective-permute-start(bf16[7,64,128]{2,1,0:T(8,128)(2,1)S(1)} %get-tuple-element.43.refs_3_.refs_0_.refs_7_), channel_id=1, source_target_pairs={{0,4},{4,0},{8,12},{12,8},{1,5},{5,1},{9,13},{13,9},{2,6},{6,2},{1... | collective-permute-start | bytes 344072 | tf_op jit(solution)/shard_map/ppermute | solution.py:44
  27.9 3.1 %collective-permute-start.5 = (bf16[7,64,128]{2,1,0:T(8,128)(2,1)S(1)}, bf16[7,64,128]{2,1,0:T(8,128)(2,1)S(1)}, u32[]{:S(2)}, u32[]{:S(2)}) collective-permute-start(bf16[7,64,128]{2,1,0:T(8,128)(2,1)S(1)} %get-tuple-element.43.refs_3_.refs_0_.refs_7_), channel_id=1, source_target_pairs={{0,1},{1,0},{2,3},{3,2},{4,8},{5,9},{6,10},{7,11},{8,4},{9,5},{10,... | collective-permute-start | bytes 344072 | tf_op jit(solution)/shard_map/ppermute | solution.py:57
  31.1 2.3 %collective-permute-start.8 = (bf16[3,7,64,128]{3,2,1,0:T(8,128)(2,1)S(1)}, bf16[3,7,64,128]{3,2,1,0:T(8,128)(2,1)S(1)}, u32[]{:S(2)}, u32[]{:S(2)}) collective-permute-start(bf16[3,7,64,128]{3,2,1,0:T(8,128)(2,1)S(1)} %shard_map.116), channel_id=1, source_target_pairs={{0,1},{1,0},{2,3},{3,2},{4,5},{5,4},{6,7},{7,6},{8,9},{9,8},{10,11... | collective-permute-start | bytes 1032200 | tf_op jit(solution)/shard_map/ppermute | solution.py:44
  32.1 6.9 %collective-permute-start.7 = (bf16[3,7,64,128]{3,2,1,0:T(8,128)(2,1)S(1)}, bf16[3,7,64,128]{3,2,1,0:T(8,128)(2,1)S(1)}, u32[]{:S(2)}, u32[]{:S(2)}) collective-permute-start(bf16[3,7,64,128]{3,2,1,0:T(8,128)(2,1)S(1)} %shard_map.116), channel_id=1, source_target_pairs={{0,16},{1,2},{2,1},{3,19},{4,20},{5,6},{6,5},{7,23},{8,24},{9,10},... | collective-permute-start | bytes 1032200 | tf_op jit(solution)/shard_map/ppermute | solution.py:57
where the time goes:
time: 43.6 us; the launch traced here: 43.3 us
  Pallas kernels  20.4 us (47%)
  starting transfers between devices  12.8 us (29%)
  waiting for transfers between devices  10.1 us (23%)
    pallas_call x6, Pallas kernels, gather_call(): pl.pallas_call(body, out_shape=tuple(outs), in_specs=[scalars(), scalars(...  18.7 us
    ppermute x4, starting transfers between devices, partner(): return lax.ppermute(block, axis, [(i, i ^ 1) for i in range(count)])  6.16 us
    ppermute x4, waiting for transfers between devices, whole_swap(): return lax.ppermute(block, axes, pairs)  5.84 us
    ppermute x4, starting transfers between devices, whole_swap(): return lax.ppermute(block, axes, pairs)  4.48 us
    ppermute x1, waiting for transfers between devices, local(): other = lax.ppermute(packed, 'gx', [(0, 1), (1, 0)])  2.76 us
    ppermute x1, starting transfers between devices, local(): other = lax.ppermute(packed, 'gx', [(0, 1), (1, 0)])  2.12 us
    ppermute x4, waiting for transfers between devices, partner(): return lax.ppermute(block, axis, [(i, i ^ 1) for i in range(count)])  1.46 us
    pallas_call x1, Pallas kernels, pack(): pl.pallas_call(body, out_shape=(jax.ShapeDtypeStruct((rows, width + HEAD,...  0.96 us
  transfers between devices with their start and end apart: 9, of which 5 were waited for; matrix products, arithmetic and copies ran while one was open for 0% of the time, Pallas kernels for 24%

commit v1 on v0

--- a/solution.py
+++ b/solution.py
@@ -216,19 +216,24 @@
     )(ints, mine, other)
 
 
-def stacked(blocks):
-    def body(*refs):
-        for k in range(len(blocks)):
-            for row in range(blocks[0].shape[0]):
-                refs[-1][k, row] = refs[k][row]
+def stacked(block, up, down):
+    def body(block_ref, up_ref, down_ref, trio_ref, rims_ref):
+        for row in range(block.shape[0]):
+            trio_ref[0, row] = block_ref[row]
+            for k, ref in enumerate((up_ref, down_ref)):
+                value = ref[row]
+                trio_ref[k + 1, row] = value
+                rims_ref[k, row] = value
 
     return pl.pallas_call(
         body,
-        out_shape=jax.ShapeDtypeStruct((len(blocks),) + blocks[0].shape, blocks[0].dtype),
-        in_specs=[whole()] * len(blocks),
-        out_specs=whole(),
+        out_shape=tuple(
+            jax.ShapeDtypeStruct((count,) + block.shape, block.dtype) for count in (3, 2)
+        ),
+        in_specs=[whole()] * 3,
+        out_specs=(whole(), whole()),
         compiler_params=params(),
-    )(*blocks)
+    )(block, up, down)
 
 
 def centre_terms(place, along, row8, spread):
@@ -566,17 +571,18 @@
         (2, 0, 0, 1, ()),
         (2, 1, -1, 1, (FAR_Y,)),
         (2, 2, 1, 1, ()),
+        (3, None, 0, -1, (FAR_Z,)),
     ]
     cross = [
-        (0, 0, 0, -1, (FAR_Z,)),
-        (0, 1, -1, -1, (FAR_Y, FAR_Z)),
-        (0, 2, 1, -1, (FAR_Z,)),
+        (0, 0, -1, -1, (FAR_Y, FAR_Z)),
+        (0, 1, 1, -1, (FAR_Z,)),
     ]
     up_turned = jnp.transpose(up_weight, (0, 2, 1))
 
     def layer_of(level, block, known, out_rows):
         up = whole_swap(block, other_y)
         down = partner(block, "gy")
+        beyond = whole_swap(block, other_z)
         right, near0, near1, near2 = known
         made = gather_call(
             0,
@@ -596,12 +602,12 @@
         if level == 0:
             right, near0 = made[:2]
         ready = made[-4:]
-        acc, up, down = lax.optimization_barrier((acc, up, down))
-        trio = stacked([block, up, down])
+        acc, up, down, beyond = lax.optimization_barrier((acc, up, down, beyond))
+        trio, rims = stacked(block, up, down)
         close = partner(trio, "gz")
-        far = whole_swap(trio, other_z)
+        far = whole_swap(rims, other_z)
         made = gather_call(
-            1, level, ints, flts, sides, frame, [up, down, close], right, near1, acc, [], out_rows
+            1, level, ints, flts, sides, frame, [up, down, close, beyond], right, near1, acc, [], out_rows
         )
         acc = made[0]
         if level == 0:

time: 43.6 us -> 42.3 us (0.970)
  Pallas kernels: 20.4 us -> 16.4 us
  starting transfers between devices: 12.8 us -> 14.5 us
  waiting for transfers between devices: 10.1 us -> 10.7 us
    pallas_call x6, Pallas kernels: 18.7 us -> 14.7 us  [gather_call(): pl.pallas_call(body, out_shape=tuple(outs), in_specs=[scalars(), scalars(...]
    ppermute x4, waiting for transfers between devices: 1.46 us -> 3.72 us  [partner(): return lax.ppermute(block, axis, [(i, i ^ 1) for i in range(count)])]
    ppermute x4 -> x6, starting transfers between devices: 4.48 us -> 6.17 us  [whole_swap(): return lax.ppermute(block, axes, pairs)]
    ppermute x4 -> x6, waiting for transfers between devices: 5.84 us -> 4.21 us  [whole_swap(): return lax.ppermute(block, axes, pairs)]
  transfers between devices with their start and end apart: 9 -> 11, of which waited for: 5 -> 6; matrix products, arithmetic and copies ran while one was open for 0% -> 0% of each run, Pallas kernels for 24% -> 21%
where the time goes in v1:
time: 42.3 us; the launch traced here: 41.7 us
  Pallas kernels  16.4 us (39%)
  starting transfers between devices  14.5 us (34%)
  waiting for transfers between devices  10.7 us (25%)
    pallas_call x6, Pallas kernels, gather_call(): pl.pallas_call(body, out_shape=tuple(outs), in_specs=[scalars(), scalars(...  14.7 us
    ppermute x4, starting transfers between devices, partner(): return lax.ppermute(block, axis, [(i, i ^ 1) for i in range(count)])  6.23 us
    ppermute x6, starting transfers between devices, whole_swap(): return lax.ppermute(block, axes, pairs)  6.17 us
    ppermute x6, waiting for transfers between devices, whole_swap(): return lax.ppermute(block, axes, pairs)  4.21 us
    ppermute x4, waiting for transfers between devices, partner(): return lax.ppermute(block, axis, [(i, i ^ 1) for i in range(count)])  3.72 us
    ppermute x1, waiting for transfers between devices, local(): other = lax.ppermute(packed, 'gx', [(0, 1), (1, 0)])  2.76 us
    ppermute x1, starting transfers between devices, local(): other = lax.ppermute(packed, 'gx', [(0, 1), (1, 0)])  2.12 us
    pallas_call x1, Pallas kernels, pack(): pl.pallas_call(body, out_shape=(jax.ShapeDtypeStruct((rows, width + HEAD,...  0.96 us
  transfers between devices with their start and end apart: 11, of which 6 were waited for; matrix products, arithmetic and copies ran while one was open for 0% of the time, Pallas kernels for 21%

profile of v1, /device:TPU:1, one launch (start us, length us, event | category | flops | bytes accessed | tf_op | source)
XLA Modules:
  0.0 41.7 jit_solution(13383955756256799725)
XLA Ops:
  0.0 1.0 %shard_map.109 = (bf16[6,72,128]{2,1,0:T(8,128)(2,1)S(1)}, s32[1,128]{1,0:T(1,128)S(1)}, f32[1,128]{1,0:T(1,128)S(1)}) custom-call(bf16[8,1,1,64,128]{4,3,2,1,0:T(8,128)(2,1)} %feat_ref.1, bf16[3,8,128]{2,1,0:T(8,128)(2,1)} %bitcast.10, s32[8]{0:T(128)} %bitcast.11, s32[3]{0:T(128)} %old_in.1, s32[3]{0:T(128)} %new_in.1, f32[2,2]{1,0:T(2,128)} %rate_in.1), custom_call_target="tpu_custom_call" | custom-call | tf_op jit(solution)/shard_map/pallas_call | solution.py:172
  1.0 2.1 %collective-permute-start = (bf16[6,72,128]{2,1,0:T(8,128)(2,1)S(1)}, bf16[6,72,128]{2,1,0:T(8,128)(2,1)S(1)}, u32[]{:S(2)}, u32[]{:S(2)}) collective-permute-start(bf16[6,72,128]{2,1,0:T(8,128)(2,1)S(1)} %get-tuple-element.38.mine_ref), channel_id=1, source_target_pairs={{0,16},{16,0},{1,17},{17,1},{2,18},{18,2},{3,19},{19,3},{4,20},{20... | collective-permute-start | bytes 331784 | tf_op jit(solution)/shard_map/ppermute | solution.py:531
  3.1 2.8 %collective-permute-done.other_ref = bf16[6,72,128]{2,1,0:T(8,128)(2,1)S(1)} collective-permute-done((bf16[6,72,128]{2,1,0:T(8,128)(2,1)S(1)}, bf16[6,72,128]{2,1,0:T(8,128)(2,1)S(1)}, u32[]{:S(2)}, u32[]{:S(2)}) %collective-permute-start) | collective-permute-done | bytes 110624 | tf_op jit(solution)/shard_map/ppermute | solution.py:531
  5.9 0.6 %shard_map.110.refs_2_.refs_3_.block_ref.refs_6_ = bf16[8,72,128]{2,1,0:T(8,128)(2,1)S(1)} custom-call(s32[1,128]{1,0:T(1,128)S(1)} %get-tuple-element.36.int_ref.refs_0_, bf16[6,72,128]{2,1,0:T(8,128)(2,1)S(1)} %get-tuple-element.38.mine_ref, bf16[6,72,128]{2,1,0:T(8,128)(2,1)S(1)} %collective-permute-done.other_ref), custom_call_target="tpu_custom_call" | custom-call | tf_op jit(solution)/shard_map/pallas_call | solution.py:210
  6.5 2.6 %collective-permute-start.3 = (bf16[8,72,128]{2,1,0:T(8,128)(2,1)S(1)}, bf16[8,72,128]{2,1,0:T(8,128)(2,1)S(1)}, u32[]{:S(2)}, u32[]{:S(2)}) collective-permute-start(bf16[8,72,128]{2,1,0:T(8,128)(2,1)S(1)} %shard_map.110.refs_2_.refs_3_.block_ref.refs_6_), channel_id=1, source_target_pairs={{0,16},{1,2},{2,1},{3,19},{4,20},{5,6},{6,5},{7,23},{8,24},{9,10},... | collective-permute-start | bytes 442376 | tf_op jit(solution)/shard_map/ppermute | solution.py:57
  9.1 1.3 %collective-permute-start.2 = (bf16[8,72,128]{2,1,0:T(8,128)(2,1)S(1)}, bf16[8,72,128]{2,1,0:T(8,128)(2,1)S(1)}, u32[]{:S(2)}, u32[]{:S(2)}) collective-permute-start(bf16[8,72,128]{2,1,0:T(8,128)(2,1)S(1)} %shard_map.110.refs_2_.refs_3_.block_ref.refs_6_), channel_id=1, source_target_pairs={{0,4},{4,0},{8,12},{12,8},{1,5},{5,1},{9,13},{13,9},{2,6},{6,2},{1... | collective-permute-start | bytes 442376 | tf_op jit(solution)/shard_map/ppermute | solution.py:44
  10.4 0.7 %collective-permute-start.1 = (bf16[8,72,128]{2,1,0:T(8,128)(2,1)S(1)}, bf16[8,72,128]{2,1,0:T(8,128)(2,1)S(1)}, u32[]{:S(2)}, u32[]{:S(2)}) collective-permute-start(bf16[8,72,128]{2,1,0:T(8,128)(2,1)S(1)} %shard_map.110.refs_2_.refs_3_.block_ref.refs_6_), channel_id=1, source_target_pairs={{0,1},{1,0},{2,3},{3,2},{4,8},{5,9},{6,10},{7,11},{8,4},{9,5},{10,... | collective-permute-start | bytes 442376 | tf_op jit(solution)/shard_map/ppermute | solution.py:57
  11.1 1.9 %shard_map.111 = (f32[7,64,256]{2,1,0:T(8,128)S(1)}, f32[8,4,128,128]{3,2,1,0:T(8,128)S(1)}, f32[1,10,8,128]{3,2,1,0:T(8,128)S(1)}, bf16[64,128]{1,0:T(8,128)(2,...) custom-call(s32[1,128]{1,0:T(1,128)S(1)} %get-tuple-element.36.int_ref.refs_0_, ...), custom_call_target="tpu_custom_call" | custom-call | flops 93585408 | bytes 1376256 | tf_op jit(solution)/shard_map/pallas_call | solution.py:494
  13.1 0.0 collective-permute-done.3.refs_6_
  13.1 1.0 %collective-permute-done.2.down_ref.refs_4_ = bf16[8,72,128]{2,1,0:T(8,128)(2,1)S(1)} collective-permute-done((bf16[8,72,128]{2,1,0:T(8,128)(2,1)S(1)}, bf16[8,72,128]{2,1,0:T(8,128)(2,1)S(1)}, u32[]{:S(2)}, u32[]{:S(2)}) %collective-permute-start.2) | collective-permute-done | bytes 147488 | tf_op jit(solution)/shard_map/ppermute | solution.py:44
  14.1 0.0 collective-permute-done.1.up_ref.refs_3_
  14.1 0.1 shard_map.112
  14.2 1.3 %collective-permute-start.5 = (bf16[3,8,72,128]{3,2,1,0:T(8,128)(2,1)S(1)}, bf16[3,8,72,128]{3,2,1,0:T(8,128)(2,1)S(1)}, u32[]{:S(2)}, u32[]{:S(2)}) collective-permute-start(bf16[3,8,72,128]{3,2,1,0:T(8,128)(2,1)S(1)} %get-tuple-element.44), channel_id=1, source_target_pairs={{0,1},{1,0},{2,3},{3,2},{4,5},{5,4},{6,7},{7,6},{8,9},{9,8},{10,11... | collective-permute-start | bytes 1327112 | tf_op jit(solution)/shard_map/ppermute | solution.py:44
  15.5 0.0 collective-permute-start.4
  15.5 1.4 %collective-permute-done.5.refs_5_ = bf16[3,8,72,128]{3,2,1,0:T(8,128)(2,1)S(1)} collective-permute-done((bf16[3,8,72,128]{3,2,1,0:T(8,128)(2,1)S(1)}, bf16[3,8,72,128]{3,2,1,0:T(8,128)(2,1)S(1)}, u32[]{:S(2)}, u32[]{:S(2)}) %collective-permute-start.5) | collective-permute-done | bytes 442400 | tf_op jit(solution)/shard_map/ppermute | solution.py:44
  17.0 0.0 copy-start
  17.0 2.9 %shard_map.113 = (f32[7,64,256]{2,1,0:T(8,128)S(1)}, f32[6,10,8,128]{3,2,1,0:T(8,128)S(1)}) custom-call(s32[1,128]{1,0:T(1,128)S(1)} %get-tuple-element.36.int_ref.refs_0_, f32[1,128]{1,0:T(1,128)S(1)} %get-tuple-element.37.refs_1_, bf16[8,72,128]{2,1,0:T(8,128)(2,1)S(1)} %shard_map.110.refs_2_.refs_3_.block_ref.refs_6_, ...), custom_call_target="tpu_custom_call" | custom-call | flops 561512448 | bytes 8257536 | tf_op jit(solution)/shard_map/pallas_call | solution.py:494
  19.9 2.1 %collective-permute-done.4.refs_3_ = bf16[2,8,72,128]{3,2,1,0:T(8,128)(2,1)S(1)} collective-permute-done((bf16[2,8,72,128]{3,2,1,0:T(8,128)(2,1)S(1)}, bf16[2,8,72,128]{3,2,1,0:T(8,128)(2,1)S(1)}, u32[]{:S(2)}, u32[]{:S(2)}) %collective-permute-start.4) | collective-permute-done | bytes 294944 | tf_op jit(solution)/shard_map/ppermute | solution.py:57
  21.9 0.0 copy-done
  21.9 2.9 %shard_map.114 = (bf16[7,64,128]{2,1,0:T(8,128)(2,1)S(1)}, f32[2,10,8,128]{3,2,1,0:T(8,128)S(1)}) custom-call(s32[1,128]{1,0:T(1,128)S(1)} %get-tuple-element.36.int_ref.refs_0_, f32[1,128]{1,0:T(1,128)S(1)} %get-tuple-element.37.refs_1_, bf16[8,72,128]{2,1,0:T(8,128)(2,1)S(1)} %shard_map.110.refs_2_.refs_3_.block_ref.refs_6_, ...), custom_call_target="tpu_custom_call" | custom-call | flops 187170816 | bytes 2752512 | tf_op jit(solution)/shard_map/pallas_call | solution.py:494
  24.8 0.1 collective-permute-start.8
  24.9 2.5 %collective-permute-start.7 = (bf16[7,64,128]{2,1,0:T(8,128)(2,1)S(1)}, bf16[7,64,128]{2,1,0:T(8,128)(2,1)S(1)}, u32[]{:S(2)}, u32[]{:S(2)}) collective-permute-start(bf16[7,64,128]{2,1,0:T(8,128)(2,1)S(1)} %get-tuple-element.52.refs_3_.block_ref.refs_7_), channel_id=1, source_target_pairs={{0,4},{4,0},{8,12},{12,8},{1,5},{5,1},{9,13},{13,9},{2,6},{6,2},{1... | collective-permute-start | bytes 344072 | tf_op jit(solution)/shard_map/ppermute | solution.py:44
  27.4 2.8 %collective-permute-start.6 = (bf16[7,64,128]{2,1,0:T(8,128)(2,1)S(1)}, bf16[7,64,128]{2,1,0:T(8,128)(2,1)S(1)}, u32[]{:S(2)}, u32[]{:S(2)}) collective-permute-start(bf16[7,64,128]{2,1,0:T(8,128)(2,1)S(1)} %get-tuple-element.52.refs_3_.block_ref.refs_7_), channel_id=1, source_target_pairs={{0,1},{1,0},{2,3},{3,2},{4,8},{5,9},{6,10},{7,11},{8,4},{9,5},{10,... | collective-permute-start | bytes 344072 | tf_op jit(solution)/shard_map/ppermute | solution.py:57
  30.1 1.7 %shard_map.115 = (f32[8,64,256]{2,1,0:T(8,128)S(1)}, bf16[64,128]{1,0:T(8,128)(2,1)S(1)}, bf16[256,64]{1,0:T(8,128)(2,1)S(1)}, f32[256,256]{1,0:T(8,128)S(1)}, f32[64,256]{1,0:T(8,128)S(1)}) custom-call(s32[1,128]{1,0:T(1,128)S(1)} %get-tuple-element.36.int_ref.refs_0_, f32[1,128]{1,0:T(1,128)S(1)} %get-tuple-element.37.refs_1_, ...), custom_call_target="tpu_custom_call" | custom-call | flops 106954752 | bytes 1572864 | tf_op jit(solution)/shard_map/pallas_call | solution.py:494
  31.8 0.0 collective-permute-done.8.refs_6_
  31.8 0.0 collective-permute-done.7.down_ref.refs_4_
  31.9 0.0 collective-permute-done.6.up_ref.refs_3_
  31.9 0.1 shard_map.116
  31.9 1.1 %collective-permute-start.10 = (bf16[3,7,64,128]{3,2,1,0:T(8,128)(2,1)S(1)}, bf16[3,7,64,128]{3,2,1,0:T(8,128)(2,1)S(1)}, u32[]{:S(2)}, u32[]{:S(2)}) collective-permute-start(bf16[3,7,64,128]{3,2,1,0:T(8,128)(2,1)S(1)} %get-tuple-element.59), channel_id=1, source_target_pairs={{0,1},{1,0},{2,3},{3,2},{4,5},{5,4},{6,7},{7,6},{8,9},{9,8},{10,11... | collective-permute-start | bytes 1032200 | tf_op jit(solution)/shard_map/ppermute | solution.py:44
  33.0 0.0 collective-permute-start.9
  33.0 1.3 %collective-permute-done.10.refs_5_ = bf16[3,7,64,128]{3,2,1,0:T(8,128)(2,1)S(1)} collective-permute-done((bf16[3,7,64,128]{3,2,1,0:T(8,128)(2,1)S(1)}, bf16[3,7,64,128]{3,2,1,0:T(8,128)(2,1)S(1)}, u32[]{:S(2)}, u32[]{:S(2)}) %collective-permute-start.10) | collective-permute-done | bytes 344096 | tf_op jit(solution)/shard_map/ppermute | solution.py:44
  34.3 2.3 %shard_map.117.refs_6_ = f32[8,64,256]{2,1,0:T(8,128)S(1)} custom-call(s32[1,128]{1,0:T(1,128)S(1)} %get-tuple-element.36.int_ref.refs_0_, f32[1,128]{1,0:T(1,128)S(1)} %get-tuple-element.37.refs_1_, bf16[8,72,128]{2,1,0:T(8,128)(2,1)S(1)} %shard_map.110.refs_2_.refs_3_.block_ref.refs_6_, bf16[7,64,128]{2,1,0:T(8,128)(2,1)S(1)} %collective-permute-done.6.up_ref.refs_3_, ...), custom_call_target="tpu_custom_call" | custom-call | flops 641728512 | bytes 9437184 | tf_op jit(solution)/shard_map/pallas_call | solution.py:494
  36.6 2.1 %collective-permute-done.9.refs_3_ = bf16[2,7,64,128]{3,2,1,0:T(8,128)(2,1)S(1)} collective-permute-done((bf16[2,7,64,128]{3,2,1,0:T(8,128)(2,1)S(1)}, bf16[2,7,64,128]{3,2,1,0:T(8,128)(2,1)S(1)}, u32[]{:S(2)}, u32[]{:S(2)}) %collective-permute-start.9) | collective-permute-done | bytes 229408 | tf_op jit(solution)/shard_map/ppermute | solution.py:57
  38.8 3.0 %shard_map.118 = bf16[8,64,128]{2,1,0:T(8,128)(2,1)} custom-call(s32[1,128]{1,0:T(1,128)S(1)} %get-tuple-element.36.int_ref.refs_0_, f32[1,128]{1,0:T(1,128)S(1)} %get-tuple-element.37.refs_1_, bf16[8,72,128]{2,1,0:T(8,128)(2,1)S(1)} %shard_map.110.refs_2_.refs_3_.block_ref.refs_6_, bf16[2,7,64,128]{3,2,1,0:T(8,128)(2,1)S(1)} %collective-permute-done.9.refs_3_, ...), custom_call_target="tpu_custom_call" | custom-call | flops 213909504 | bytes 3145728 | tf_op jit(solution)/shard_map/pallas_call | solution.py:494
Async XLA Ops:
  1.0 4.9 %collective-permute-start = (bf16[6,72,128]{2,1,0:T(8,128)(2,1)S(1)}, bf16[6,72,128]{2,1,0:T(8,128)(2,1)S(1)}, u32[]{:S(2)}, u32[]{:S(2)}) collective-permute-start(bf16[6,72,128]{2,1,0:T(8,128)(2,1)S(1)} %get-tuple-element.38.mine_ref), channel_id=1, source_target_pairs={{0,16},{16,0},{1,17},{17,1},{2,18},{18,2},{3,19},{19,3},{4,20},{20... | collective-permute-start | bytes 331784 | tf_op jit(solution)/shard_map/ppermute | solution.py:531
  6.5 6.6 %collective-permute-start.3 = (bf16[8,72,128]{2,1,0:T(8,128)(2,1)S(1)}, bf16[8,72,128]{2,1,0:T(8,128)(2,1)S(1)}, u32[]{:S(2)}, u32[]{:S(2)}) collective-permute-start(bf16[8,72,128]{2,1,0:T(8,128)(2,1)S(1)} %shard_map.110.refs_2_.refs_3_.block_ref.refs_6_), channel_id=1, source_target_pairs={{0,16},{1,2},{2,1},{3,19},{4,20},{5,6},{6,5},{7,23},{8,24},{9,10},... | collective-permute-start | bytes 442376 | tf_op jit(solution)/shard_map/ppermute | solution.py:57
  9.1 5.0 %collective-permute-start.2 = (bf16[8,72,128]{2,1,0:T(8,128)(2,1)S(1)}, bf16[8,72,128]{2,1,0:T(8,128)(2,1)S(1)}, u32[]{:S(2)}, u32[]{:S(2)}) collective-permute-start(bf16[8,72,128]{2,1,0:T(8,128)(2,1)S(1)} %shard_map.110.refs_2_.refs_3_.block_ref.refs_6_), channel_id=1, source_target_pairs={{0,4},{4,0},{8,12},{12,8},{1,5},{5,1},{9,13},{13,9},{2,6},{6,2},{1... | collective-permute-start | bytes 442376 | tf_op jit(solution)/shard_map/ppermute | solution.py:44
  10.4 3.7 %collective-permute-start.1 = (bf16[8,72,128]{2,1,0:T(8,128)(2,1)S(1)}, bf16[8,72,128]{2,1,0:T(8,128)(2,1)S(1)}, u32[]{:S(2)}, u32[]{:S(2)}) collective-permute-start(bf16[8,72,128]{2,1,0:T(8,128)(2,1)S(1)} %shard_map.110.refs_2_.refs_3_.block_ref.refs_6_), channel_id=1, source_target_pairs={{0,1},{1,0},{2,3},{3,2},{4,8},{5,9},{6,10},{7,11},{8,4},{9,5},{10,... | collective-permute-start | bytes 442376 | tf_op jit(solution)/shard_map/ppermute | solution.py:57
  14.2 2.8 %collective-permute-start.5 = (bf16[3,8,72,128]{3,2,1,0:T(8,128)(2,1)S(1)}, bf16[3,8,72,128]{3,2,1,0:T(8,128)(2,1)S(1)}, u32[]{:S(2)}, u32[]{:S(2)}) collective-permute-start(bf16[3,8,72,128]{3,2,1,0:T(8,128)(2,1)S(1)} %get-tuple-element.44), channel_id=1, source_target_pairs={{0,1},{1,0},{2,3},{3,2},{4,5},{5,4},{6,7},{7,6},{8,9},{9,8},{10,11... | collective-permute-start | bytes 1327112 | tf_op jit(solution)/shard_map/ppermute | solution.py:44
  15.5 6.4 %collective-permute-start.4 = (bf16[2,8,72,128]{3,2,1,0:T(8,128)(2,1)S(1)}, bf16[2,8,72,128]{3,2,1,0:T(8,128)(2,1)S(1)}, u32[]{:S(2)}, u32[]{:S(2)}) collective-permute-start(bf16[2,8,72,128]{3,2,1,0:T(8,128)(2,1)S(1)} %get-tuple-element.42), channel_id=1, source_target_pairs={{0,16},{1,2},{2,1},{3,19},{4,20},{5,6},{6,5},{7,23},{8,24},{9,10},... | collective-permute-start | bytes 884744 | tf_op jit(solution)/shard_map/ppermute | solution.py:57
  17.0 5.0 %copy-start = (bf16[2,64,256]{2,1,0:T(8,128)(2,1)S(1)}, bf16[2,64,256]{2,1,0:T(8,128)(2,1)}, u32[]{:S(2)}) copy-start(bf16[2,64,256]{2,1,0:T(8,128)(2,1)} %refs_8_.3) | copy-start | bytes 196612
  24.8 7.0 %collective-permute-start.8 = (bf16[7,64,128]{2,1,0:T(8,128)(2,1)S(1)}, bf16[7,64,128]{2,1,0:T(8,128)(2,1)S(1)}, u32[]{:S(2)}, u32[]{:S(2)}) collective-permute-start(bf16[7,64,128]{2,1,0:T(8,128)(2,1)S(1)} %get-tuple-element.52.refs_3_.block_ref.refs_7_), channel_id=1, source_target_pairs={{0,16},{1,2},{2,1},{3,19},{4,20},{5,6},{6,5},{7,23},{8,24},{9,10},... | collective-permute-start | bytes 344072 | tf_op jit(solution)/shard_map/ppermute | solution.py:57
  24.9 7.0 %collective-permute-start.7 = (bf16[7,64,128]{2,1,0:T(8,128)(2,1)S(1)}, bf16[7,64,128]{2,1,0:T(8,128)(2,1)S(1)}, u32[]{:S(2)}, u32[]{:S(2)}) collective-permute-start(bf16[7,64,128]{2,1,0:T(8,128)(2,1)S(1)} %get-tuple-element.52.refs_3_.block_ref.refs_7_), channel_id=1, source_target_pairs={{0,4},{4,0},{8,12},{12,8},{1,5},{5,1},{9,13},{13,9},{2,6},{6,2},{1... | collective-permute-start | bytes 344072 | tf_op jit(solution)/shard_map/ppermute | solution.py:44
  27.4 4.5 %collective-permute-start.6 = (bf16[7,64,128]{2,1,0:T(8,128)(2,1)S(1)}, bf16[7,64,128]{2,1,0:T(8,128)(2,1)S(1)}, u32[]{:S(2)}, u32[]{:S(2)}) collective-permute-start(bf16[7,64,128]{2,1,0:T(8,128)(2,1)S(1)} %get-tuple-element.52.refs_3_.block_ref.refs_7_), channel_id=1, source_target_pairs={{0,1},{1,0},{2,3},{3,2},{4,8},{5,9},{6,10},{7,11},{8,4},{9,5},{10,... | collective-permute-start | bytes 344072 | tf_op jit(solution)/shard_map/ppermute | solution.py:57
  31.9 2.4 %collective-permute-start.10 = (bf16[3,7,64,128]{3,2,1,0:T(8,128)(2,1)S(1)}, bf16[3,7,64,128]{3,2,1,0:T(8,128)(2,1)S(1)}, u32[]{:S(2)}, u32[]{:S(2)}) collective-permute-start(bf16[3,7,64,128]{3,2,1,0:T(8,128)(2,1)S(1)} %get-tuple-element.59), channel_id=1, source_target_pairs={{0,1},{1,0},{2,3},{3,2},{4,5},{5,4},{6,7},{7,6},{8,9},{9,8},{10,11... | collective-permute-start | bytes 1032200 | tf_op jit(solution)/shard_map/ppermute | solution.py:44
  33.0 5.7 %collective-permute-start.9 = (bf16[2,7,64,128]{3,2,1,0:T(8,128)(2,1)S(1)}, bf16[2,7,64,128]{3,2,1,0:T(8,128)(2,1)S(1)}, u32[]{:S(2)}, u32[]{:S(2)}) collective-permute-start(bf16[2,7,64,128]{3,2,1,0:T(8,128)(2,1)S(1)} %get-tuple-element.57), channel_id=1, source_target_pairs={{0,16},{1,2},{2,1},{3,19},{4,20},{5,6},{6,5},{7,23},{8,24},{9,10},... | collective-permute-start | bytes 688136 | tf_op jit(solution)/shard_map/ppermute | solution.py:57

commit v2 on v1

--- a/solution.py
+++ b/solution.py
@@ -12,6 +12,7 @@
 LOG2E = math.log2(math.e)
 HEAD = 8
 TERMS = 32
+REACH = 3
 VMEM_LIMIT = 32 * 2**20
 
 MID_START, MID_STOP, LOW, HIGH, MID_AT, OUT_START, OUT_STOP, CUT, COLUMN = range(9)
@@ -95,6 +96,7 @@
         new_in,
         rate_in,
         out_ref,
+        edge_ref,
         int_ref,
         flt_ref,
         pos_ref,
@@ -167,17 +169,21 @@
             block = jnp.concatenate(place + [far, spare], axis=0).astype(jnp.bfloat16)
             out_ref[row, width : width + HEAD, :] = block
         copies[5].wait()
+        first = jnp.where(column == 0, jnp.maximum(old_ref[1] - REACH, 0), 0)
+        for k in range(REACH):
+            edge_ref[k] = out_ref[jnp.minimum(first + k, rows - 1)]
 
     anywhere = pl.BlockSpec(memory_space=pltpu.HBM)
     return pl.pallas_call(
         body,
         out_shape=(
             jax.ShapeDtypeStruct((rows, width + HEAD, slots), jnp.bfloat16),
+            jax.ShapeDtypeStruct((REACH, width + HEAD, slots), jnp.bfloat16),
             jax.ShapeDtypeStruct((1, slots), jnp.int32),
             jax.ShapeDtypeStruct((1, slots), jnp.float32),
         ),
         in_specs=[anywhere] * 6,
-        out_specs=(whole(), whole(), whole()),
+        out_specs=(whole(), whole(), whole(), whole()),
         scratch_shapes=[
             pltpu.VMEM((3, slot_rows, slots), positions.dtype),
             pltpu.SMEM((slot_rows,), counts.dtype),
@@ -200,12 +206,12 @@
 def assemble(ints, mine, other, rows):
     def body(int_ref, mine_ref, other_ref, out_ref):
         cut, column = int_ref[0, CUT], int_ref[0, COLUMN]
+        begin = jnp.where(column == 0, cut, jnp.maximum(cut - REACH, 0))
         for row in range(rows):
-            owner = jnp.int32(row) >= cut
-            place = jnp.where(owner, row - cut, row)
-            place = jnp.clip(place, 0, mine_ref.shape[0] - 1)
-            is_mine = owner.astype(jnp.int32) == column
-            out_ref[row] = jnp.where(is_mine, mine_ref[place], other_ref[place])
+            owner = (jnp.int32(row) >= cut).astype(jnp.int32)
+            place = jnp.clip(row - owner * cut, 0, mine_ref.shape[0] - 1)
+            there = jnp.clip(row - begin, 0, REACH - 1)
+            out_ref[row] = jnp.where(owner == column, mine_ref[place], other_ref[there])
 
     return pl.pallas_call(
         body,
@@ -423,8 +429,8 @@
                 wconv_ref[...] = jnp.concatenate(
                     [conv_in[level, :, m, :] for m in range(2)], axis=1
                 )
-                wup_ref[...] = up_ref[level].astype(jnp.float32).T.astype(jnp.bfloat16)
-                lift = jnp.broadcast_to(upb_ref[level : level + 1, :], (slots, upb_ref.shape[1])).T
+                wup_ref[...] = (0.5 * up_ref[level].astype(jnp.float32)).T.astype(jnp.bfloat16)
+                lift = 0.5 * jnp.broadcast_to(upb_ref[level : level + 1, :], (slots, upb_ref.shape[1])).T
                 wupb_ref[...] = jnp.concatenate([lift, lift], axis=1)
                 low = jnp.broadcast_to(downb_ref[level : level + 1, :], (slots, features))
                 low = jnp.concatenate([low, low], axis=1).T[0:features, :]
@@ -443,7 +449,7 @@
             spread = jnp.mean(centred * centred, axis=0, keepdims=True)
             normed = (centred * lax.rsqrt(spread + EPSILON)).astype(jnp.bfloat16)
             hidden = jnp.dot(wup_ref[...], normed, preferred_element_type=jnp.float32)
-            half = 0.5 * (hidden + wupb_ref[:, 0:size])
+            half = hidden + wupb_ref[:, 0:size]
             hidden = (half + half * jnp.tanh(half)).astype(jnp.bfloat16)
             update = jnp.dot(down_ref[level], hidden, preferred_element_type=jnp.float32)
             update = update + wdownb_ref[:, 0:size]
@@ -523,12 +529,12 @@
     slot_rows = features.shape[0]
     total = peers * slot_rows // 2
     most = min(slot_rows, total - 2 * (peers - 1))
-    packed, ints, flts = pack(
+    packed, edge, ints, flts = pack(
         features, positions, counts, old_cuts, new_cuts, radial_rates, most
     )
 
     if peers == 2:
-        other = lax.ppermute(packed, "gx", [(0, 1), (1, 0)])
+        other = lax.ppermute(edge, "gx", [(0, 1), (1, 0)])
         frame = assemble(ints, packed, other, total)
         mid_rows = total - 1
     else:
@@ -540,7 +546,7 @@
         base = new_cuts[column] - 2
         pieces = [packed]
         starts = [old_low]
-        for by, rows in ((1, 3), (2, 1)):
+        for by, rows in ((1, REACH), (2, 1)):
             tail_at = jnp.maximum(held - rows, 0)
             tail = lax.dynamic_slice_in_dim(packed, tail_at, rows, 0)
             pieces.append(shift(tail, "gx", by))

time: 42.3 us -> 41.8 us (0.988)
  waiting for transfers between devices: 10.7 us -> 6.28 us
  Pallas kernels: 16.4 us -> 20.7 us
    pallas_call x6, Pallas kernels: 14.7 us -> 18.9 us  [gather_call(): pl.pallas_call(body, out_shape=tuple(outs), in_specs=[scalars(), scalars(...]
    ppermute x6, waiting for transfers between devices: 4.21 us -> 1.98 us  [whole_swap(): return lax.ppermute(block, axes, pairs)]
    ppermute x1, waiting for transfers between devices: 2.76 us -> 1.55 us  [local(): other = lax.ppermute(edge, 'gx', [(0, 1), (1, 0)])]
    ppermute x4, waiting for transfers between devices: 3.72 us -> 2.75 us  [partner(): return lax.ppermute(block, axis, [(i, i ^ 1) for i in range(count)])]
    ppermute x6, starting transfers between devices: 6.17 us -> 5.7 us  [whole_swap(): return lax.ppermute(block, axes, pairs)]
  transfers between devices with their start and end apart: 11 -> 11, of which waited for: 6 -> 6; matrix products, arithmetic and copies ran while one was open for 0% -> 0% of each run, Pallas kernels for 21% -> 27%
where the time goes in v2:
time: 41.8 us; the launch traced here: 41.4 us
  Pallas kernels  20.7 us (50%)
  starting transfers between devices  14.3 us (34%)
  waiting for transfers between devices  6.28 us (15%)
    pallas_call x6, Pallas kernels, gather_call(): pl.pallas_call(body, out_shape=tuple(outs), in_specs=[scalars(), scalars(...  18.9 us
    ppermute x4, starting transfers between devices, partner(): return lax.ppermute(block, axis, [(i, i ^ 1) for i in range(count)])  6.51 us
    ppermute x6, starting transfers between devices, whole_swap(): return lax.ppermute(block, axes, pairs)  5.7 us
    ppermute x4, waiting for transfers between devices, partner(): return lax.ppermute(block, axis, [(i, i ^ 1) for i in range(count)])  2.75 us
    ppermute x1, starting transfers between devices, local(): other = lax.ppermute(edge, 'gx', [(0, 1), (1, 0)])  2.12 us
    ppermute x6, waiting for transfers between devices, whole_swap(): return lax.ppermute(block, axes, pairs)  1.98 us
    ppermute x1, waiting for transfers between devices, local(): other = lax.ppermute(edge, 'gx', [(0, 1), (1, 0)])  1.55 us
    pallas_call x1, Pallas kernels, pack(): pl.pallas_call(body, out_shape=(jax.ShapeDtypeStruct((rows, width + HEAD,...  0.97 us
  transfers between devices with their start and end apart: 11, of which 6 were waited for; matrix products, arithmetic and copies ran while one was open for 0% of the time, Pallas kernels for 27%

profile of v2, /device:TPU:1, one launch (start us, length us, event | category | flops | bytes accessed | tf_op | source)
XLA Modules:
  0.0 41.4 jit_solution(16552240631962551100)
XLA Ops:
  0.0 1.0 %shard_map.109 = (bf16[6,72,128]{2,1,0:T(8,128)(2,1)S(1)}, bf16[3,72,128]{2,1,0:T(8,128)(2,1)S(1)}, s32[1,128]{1,0:T(1,128)S(1)}, f32[1,128]{1,0:T(1,128)S(1)}) custom-call(bf16[8,1,1,64,128]{4,3,2,1,0:T(8,128)(2,1)} %feat_ref.1, bf16[3,8,128]{2,1,0:T(8,128)(2,1)} %bitcast.10, s32[8]{0:T(128)} %bitcast.11, s32[3]{0:T(128)} %old_in.1, s32[3]{0:T(128)} %new_in.1, ...), custom_call_target="tpu_custom_call" | custom-call | tf_op jit(solution)/shard_map/pallas_call | solution.py:177
  1.0 2.1 %collective-permute-start = (bf16[3,72,128]{2,1,0:T(8,128)(2,1)S(1)}, bf16[3,72,128]{2,1,0:T(8,128)(2,1)S(1)}, u32[]{:S(2)}, u32[]{:S(2)}) collective-permute-start(bf16[3,72,128]{2,1,0:T(8,128)(2,1)S(1)} %get-tuple-element.40), channel_id=1, source_target_pairs={{0,16},{16,0},{1,17},{17,1},{2,18},{18,2},{3,19},{19,3},{4,20},{20... | collective-permute-start | bytes 165896 | tf_op jit(solution)/shard_map/ppermute | solution.py:537
  3.1 1.5 %collective-permute-done.other_ref = bf16[3,72,128]{2,1,0:T(8,128)(2,1)S(1)} collective-permute-done((bf16[3,72,128]{2,1,0:T(8,128)(2,1)S(1)}, bf16[3,72,128]{2,1,0:T(8,128)(2,1)S(1)}, u32[]{:S(2)}, u32[]{:S(2)}) %collective-permute-start) | collective-permute-done | bytes 55328 | tf_op jit(solution)/shard_map/ppermute | solution.py:537
  4.6 0.6 %shard_map.110.refs_2_.refs_3_.block_ref.refs_6_ = bf16[8,72,128]{2,1,0:T(8,128)(2,1)S(1)} custom-call(s32[1,128]{1,0:T(1,128)S(1)} %get-tuple-element.37.int_ref.refs_0_, bf16[6,72,128]{2,1,0:T(8,128)(2,1)S(1)} %get-tuple-element.39.mine_ref, bf16[3,72,128]{2,1,0:T(8,128)(2,1)S(1)} %collective-permute-done.other_ref), custom_call_target="tpu_custom_call" | custom-call | tf_op jit(solution)/shard_map/pallas_call | solution.py:216
  5.3 3.2 %collective-permute-start.3 = (bf16[8,72,128]{2,1,0:T(8,128)(2,1)S(1)}, bf16[8,72,128]{2,1,0:T(8,128)(2,1)S(1)}, u32[]{:S(2)}, u32[]{:S(2)}) collective-permute-start(bf16[8,72,128]{2,1,0:T(8,128)(2,1)S(1)} %shard_map.110.refs_2_.refs_3_.block_ref.refs_6_), channel_id=1, source_target_pairs={{0,16},{1,2},{2,1},{3,19},{4,20},{5,6},{6,5},{7,23},{8,24},{9,10},... | collective-permute-start | bytes 442376 | tf_op jit(solution)/shard_map/ppermute | solution.py:58
  8.5 1.3 %collective-permute-start.2 = (bf16[8,72,128]{2,1,0:T(8,128)(2,1)S(1)}, bf16[8,72,128]{2,1,0:T(8,128)(2,1)S(1)}, u32[]{:S(2)}, u32[]{:S(2)}) collective-permute-start(bf16[8,72,128]{2,1,0:T(8,128)(2,1)S(1)} %shard_map.110.refs_2_.refs_3_.block_ref.refs_6_), channel_id=1, source_target_pairs={{0,4},{4,0},{8,12},{12,8},{1,5},{5,1},{9,13},{13,9},{2,6},{6,2},{1... | collective-permute-start | bytes 442376 | tf_op jit(solution)/shard_map/ppermute | solution.py:45
  9.8 0.7 %collective-permute-start.1 = (bf16[8,72,128]{2,1,0:T(8,128)(2,1)S(1)}, bf16[8,72,128]{2,1,0:T(8,128)(2,1)S(1)}, u32[]{:S(2)}, u32[]{:S(2)}) collective-permute-start(bf16[8,72,128]{2,1,0:T(8,128)(2,1)S(1)} %shard_map.110.refs_2_.refs_3_.block_ref.refs_6_), channel_id=1, source_target_pairs={{0,1},{1,0},{2,3},{3,2},{4,8},{5,9},{6,10},{7,11},{8,4},{9,5},{10,... | collective-permute-start | bytes 442376 | tf_op jit(solution)/shard_map/ppermute | solution.py:58
  10.5 2.3 %shard_map.111 = (f32[7,64,256]{2,1,0:T(8,128)S(1)}, f32[8,4,128,128]{3,2,1,0:T(8,128)S(1)}, f32[1,10,8,128]{3,2,1,0:T(8,128)S(1)}, bf16[64,128]{1,0:T(8,128)(2,...) custom-call(s32[1,128]{1,0:T(1,128)S(1)} %get-tuple-element.37.int_ref.refs_0_, ...), custom_call_target="tpu_custom_call" | custom-call | flops 93585408 | bytes 1376256 | tf_op jit(solution)/shard_map/pallas_call | solution.py:500
  12.7 0.0 collective-permute-done.3.refs_6_
  12.8 0.7 %collective-permute-done.2.down_ref.refs_4_ = bf16[8,72,128]{2,1,0:T(8,128)(2,1)S(1)} collective-permute-done((bf16[8,72,128]{2,1,0:T(8,128)(2,1)S(1)}, bf16[8,72,128]{2,1,0:T(8,128)(2,1)S(1)}, u32[]{:S(2)}, u32[]{:S(2)}) %collective-permute-start.2) | collective-permute-done | bytes 147488 | tf_op jit(solution)/shard_map/ppermute | solution.py:45
  13.5 0.0 collective-permute-done.1.up_ref.refs_3_
  13.5 0.1 shard_map.112
  13.6 1.3 %collective-permute-start.5 = (bf16[3,8,72,128]{3,2,1,0:T(8,128)(2,1)S(1)}, bf16[3,8,72,128]{3,2,1,0:T(8,128)(2,1)S(1)}, u32[]{:S(2)}, u32[]{:S(2)}) collective-permute-start(bf16[3,8,72,128]{3,2,1,0:T(8,128)(2,1)S(1)} %get-tuple-element.46), channel_id=1, source_target_pairs={{0,1},{1,0},{2,3},{3,2},{4,5},{5,4},{6,7},{7,6},{8,9},{9,8},{10,11... | collective-permute-start | bytes 1327112 | tf_op jit(solution)/shard_map/ppermute | solution.py:45
  14.9 0.0 collective-permute-start.4
  14.9 1.4 %collective-permute-done.5.refs_5_ = bf16[3,8,72,128]{3,2,1,0:T(8,128)(2,1)S(1)} collective-permute-done((bf16[3,8,72,128]{3,2,1,0:T(8,128)(2,1)S(1)}, bf16[3,8,72,128]{3,2,1,0:T(8,128)(2,1)S(1)}, u32[]{:S(2)}, u32[]{:S(2)}) %collective-permute-start.5) | collective-permute-done | bytes 442400 | tf_op jit(solution)/shard_map/ppermute | solution.py:45
  16.3 0.0 copy-start
  16.3 4.0 %shard_map.113 = (f32[7,64,256]{2,1,0:T(8,128)S(1)}, f32[6,10,8,128]{3,2,1,0:T(8,128)S(1)}) custom-call(s32[1,128]{1,0:T(1,128)S(1)} %get-tuple-element.37.int_ref.refs_0_, f32[1,128]{1,0:T(1,128)S(1)} %get-tuple-element.38.refs_1_, bf16[8,72,128]{2,1,0:T(8,128)(2,1)S(1)} %shard_map.110.refs_2_.refs_3_.block_ref.refs_6_, ...), custom_call_target="tpu_custom_call" | custom-call | flops 561512448 | bytes 8257536 | tf_op jit(solution)/shard_map/pallas_call | solution.py:500
  20.3 1.0 %collective-permute-done.4.refs_3_ = bf16[2,8,72,128]{3,2,1,0:T(8,128)(2,1)S(1)} collective-permute-done((bf16[2,8,72,128]{3,2,1,0:T(8,128)(2,1)S(1)}, bf16[2,8,72,128]{3,2,1,0:T(8,128)(2,1)S(1)}, u32[]{:S(2)}, u32[]{:S(2)}) %collective-permute-start.4) | collective-permute-done | bytes 294944 | tf_op jit(solution)/shard_map/ppermute | solution.py:58
  21.3 0.0 copy-done
  21.3 3.7 %shard_map.114 = (bf16[7,64,128]{2,1,0:T(8,128)(2,1)S(1)}, f32[2,10,8,128]{3,2,1,0:T(8,128)S(1)}) custom-call(s32[1,128]{1,0:T(1,128)S(1)} %get-tuple-element.37.int_ref.refs_0_, f32[1,128]{1,0:T(1,128)S(1)} %get-tuple-element.38.refs_1_, bf16[8,72,128]{2,1,0:T(8,128)(2,1)S(1)} %shard_map.110.refs_2_.refs_3_.block_ref.refs_6_, ...), custom_call_target="tpu_custom_call" | custom-call | flops 187170816 | bytes 2752512 | tf_op jit(solution)/shard_map/pallas_call | solution.py:500
  25.0 0.1 collective-permute-start.8
  25.1 2.5 %collective-permute-start.7 = (bf16[7,64,128]{2,1,0:T(8,128)(2,1)S(1)}, bf16[7,64,128]{2,1,0:T(8,128)(2,1)S(1)}, u32[]{:S(2)}, u32[]{:S(2)}) collective-permute-start(bf16[7,64,128]{2,1,0:T(8,128)(2,1)S(1)} %get-tuple-element.54.refs_3_.block_ref.refs_7_), channel_id=1, source_target_pairs={{0,4},{4,0},{8,12},{12,8},{1,5},{5,1},{9,13},{13,9},{2,6},{6,2},{1... | collective-permute-start | bytes 344072 | tf_op jit(solution)/shard_map/ppermute | solution.py:45
  27.6 1.0 %collective-permute-start.6 = (bf16[7,64,128]{2,1,0:T(8,128)(2,1)S(1)}, bf16[7,64,128]{2,1,0:T(8,128)(2,1)S(1)}, u32[]{:S(2)}, u32[]{:S(2)}) collective-permute-start(bf16[7,64,128]{2,1,0:T(8,128)(2,1)S(1)} %get-tuple-element.54.refs_3_.block_ref.refs_7_), channel_id=1, source_target_pairs={{0,1},{1,0},{2,3},{3,2},{4,8},{5,9},{6,10},{7,11},{8,4},{9,5},{10,... | collective-permute-start | bytes 344072 | tf_op jit(solution)/shard_map/ppermute | solution.py:58
  28.6 1.7 %shard_map.115 = (f32[8,64,256]{2,1,0:T(8,128)S(1)}, bf16[64,128]{1,0:T(8,128)(2,1)S(1)}, bf16[256,64]{1,0:T(8,128)(2,1)S(1)}, f32[256,256]{1,0:T(8,128)S(1)}, f32[64,256]{1,0:T(8,128)S(1)}) custom-call(s32[1,128]{1,0:T(1,128)S(1)} %get-tuple-element.37.int_ref.refs_0_, f32[1,128]{1,0:T(1,128)S(1)} %get-tuple-element.38.refs_1_, ...), custom_call_target="tpu_custom_call" | custom-call | flops 106954752 | bytes 1572864 | tf_op jit(solution)/shard_map/pallas_call | solution.py:500
  30.3 0.0 collective-permute-done.8.refs_6_
  30.3 0.0 collective-permute-done.7.down_ref.refs_4_
  30.4 0.0 collective-permute-done.6.up_ref.refs_3_
  30.4 0.1 shard_map.116
  30.5 1.4 %collective-permute-start.10 = (bf16[3,7,64,128]{3,2,1,0:T(8,128)(2,1)S(1)}, bf16[3,7,64,128]{3,2,1,0:T(8,128)(2,1)S(1)}, u32[]{:S(2)}, u32[]{:S(2)}) collective-permute-start(bf16[3,7,64,128]{3,2,1,0:T(8,128)(2,1)S(1)} %get-tuple-element.61), channel_id=1, source_target_pairs={{0,1},{1,0},{2,3},{3,2},{4,5},{5,4},{6,7},{7,6},{8,9},{9,8},{10,11... | collective-permute-start | bytes 1032200 | tf_op jit(solution)/shard_map/ppermute | solution.py:45
  31.9 0.7 %collective-permute-start.9 = (bf16[2,7,64,128]{3,2,1,0:T(8,128)(2,1)S(1)}, bf16[2,7,64,128]{3,2,1,0:T(8,128)(2,1)S(1)}, u32[]{:S(2)}, u32[]{:S(2)}) collective-permute-start(bf16[2,7,64,128]{3,2,1,0:T(8,128)(2,1)S(1)} %get-tuple-element.59), channel_id=1, source_target_pairs={{0,16},{1,2},{2,1},{3,19},{4,20},{5,6},{6,5},{7,23},{8,24},{9,10},... | collective-permute-start | bytes 688136 | tf_op jit(solution)/shard_map/ppermute | solution.py:58
  32.5 0.6 %collective-permute-done.10.refs_5_ = bf16[3,7,64,128]{3,2,1,0:T(8,128)(2,1)S(1)} collective-permute-done((bf16[3,7,64,128]{3,2,1,0:T(8,128)(2,1)S(1)}, bf16[3,7,64,128]{3,2,1,0:T(8,128)(2,1)S(1)}, u32[]{:S(2)}, u32[]{:S(2)}) %collective-permute-start.10) | collective-permute-done | bytes 344096 | tf_op jit(solution)/shard_map/ppermute | solution.py:45
  33.1 3.4 %shard_map.117.refs_6_ = f32[8,64,256]{2,1,0:T(8,128)S(1)} custom-call(s32[1,128]{1,0:T(1,128)S(1)} %get-tuple-element.37.int_ref.refs_0_, f32[1,128]{1,0:T(1,128)S(1)} %get-tuple-element.38.refs_1_, bf16[8,72,128]{2,1,0:T(8,128)(2,1)S(1)} %shard_map.110.refs_2_.refs_3_.block_ref.refs_6_, bf16[7,64,128]{2,1,0:T(8,128)(2,1)S(1)} %collective-permute-done.6.up_ref.refs_3_, ...), custom_call_target="tpu_custom_call" | custom-call | flops 641728512 | bytes 9437184 | tf_op jit(solution)/shard_map/pallas_call | solution.py:500
  36.6 1.0 %collective-permute-done.9.refs_3_ = bf16[2,7,64,128]{3,2,1,0:T(8,128)(2,1)S(1)} collective-permute-done((bf16[2,7,64,128]{3,2,1,0:T(8,128)(2,1)S(1)}, bf16[2,7,64,128]{3,2,1,0:T(8,128)(2,1)S(1)}, u32[]{:S(2)}, u32[]{:S(2)}) %collective-permute-start.9) | collective-permute-done | bytes 229408 | tf_op jit(solution)/shard_map/ppermute | solution.py:58
  37.6 3.8 %shard_map.118 = bf16[8,64,128]{2,1,0:T(8,128)(2,1)} custom-call(s32[1,128]{1,0:T(1,128)S(1)} %get-tuple-element.37.int_ref.refs_0_, f32[1,128]{1,0:T(1,128)S(1)} %get-tuple-element.38.refs_1_, bf16[8,72,128]{2,1,0:T(8,128)(2,1)S(1)} %shard_map.110.refs_2_.refs_3_.block_ref.refs_6_, bf16[2,7,64,128]{3,2,1,0:T(8,128)(2,1)S(1)} %collective-permute-done.9.refs_3_, ...), custom_call_target="tpu_custom_call" | custom-call | flops 213909504 | bytes 3145728 | tf_op jit(solution)/shard_map/pallas_call | solution.py:500
Async XLA Ops:
  1.0 3.7 %collective-permute-start = (bf16[3,72,128]{2,1,0:T(8,128)(2,1)S(1)}, bf16[3,72,128]{2,1,0:T(8,128)(2,1)S(1)}, u32[]{:S(2)}, u32[]{:S(2)}) collective-permute-start(bf16[3,72,128]{2,1,0:T(8,128)(2,1)S(1)} %get-tuple-element.40), channel_id=1, source_target_pairs={{0,16},{16,0},{1,17},{17,1},{2,18},{18,2},{3,19},{19,3},{4,20},{20... | collective-permute-start | bytes 165896 | tf_op jit(solution)/shard_map/ppermute | solution.py:537
  5.3 7.5 %collective-permute-start.3 = (bf16[8,72,128]{2,1,0:T(8,128)(2,1)S(1)}, bf16[8,72,128]{2,1,0:T(8,128)(2,1)S(1)}, u32[]{:S(2)}, u32[]{:S(2)}) collective-permute-start(bf16[8,72,128]{2,1,0:T(8,128)(2,1)S(1)} %shard_map.110.refs_2_.refs_3_.block_ref.refs_6_), channel_id=1, source_target_pairs={{0,16},{1,2},{2,1},{3,19},{4,20},{5,6},{6,5},{7,23},{8,24},{9,10},... | collective-permute-start | bytes 442376 | tf_op jit(solution)/shard_map/ppermute | solution.py:58
  8.5 5.0 %collective-permute-start.2 = (bf16[8,72,128]{2,1,0:T(8,128)(2,1)S(1)}, bf16[8,72,128]{2,1,0:T(8,128)(2,1)S(1)}, u32[]{:S(2)}, u32[]{:S(2)}) collective-permute-start(bf16[8,72,128]{2,1,0:T(8,128)(2,1)S(1)} %shard_map.110.refs_2_.refs_3_.block_ref.refs_6_), channel_id=1, source_target_pairs={{0,4},{4,0},{8,12},{12,8},{1,5},{5,1},{9,13},{13,9},{2,6},{6,2},{1... | collective-permute-start | bytes 442376 | tf_op jit(solution)/shard_map/ppermute | solution.py:45
  9.8 3.7 %collective-permute-start.1 = (bf16[8,72,128]{2,1,0:T(8,128)(2,1)S(1)}, bf16[8,72,128]{2,1,0:T(8,128)(2,1)S(1)}, u32[]{:S(2)}, u32[]{:S(2)}) collective-permute-start(bf16[8,72,128]{2,1,0:T(8,128)(2,1)S(1)} %shard_map.110.refs_2_.refs_3_.block_ref.refs_6_), channel_id=1, source_target_pairs={{0,1},{1,0},{2,3},{3,2},{4,8},{5,9},{6,10},{7,11},{8,4},{9,5},{10,... | collective-permute-start | bytes 442376 | tf_op jit(solution)/shard_map/ppermute | solution.py:58
  13.6 2.8 %collective-permute-start.5 = (bf16[3,8,72,128]{3,2,1,0:T(8,128)(2,1)S(1)}, bf16[3,8,72,128]{3,2,1,0:T(8,128)(2,1)S(1)}, u32[]{:S(2)}, u32[]{:S(2)}) collective-permute-start(bf16[3,8,72,128]{3,2,1,0:T(8,128)(2,1)S(1)} %get-tuple-element.46), channel_id=1, source_target_pairs={{0,1},{1,0},{2,3},{3,2},{4,5},{5,4},{6,7},{7,6},{8,9},{9,8},{10,11... | collective-permute-start | bytes 1327112 | tf_op jit(solution)/shard_map/ppermute | solution.py:45
  14.9 6.4 %collective-permute-start.4 = (bf16[2,8,72,128]{3,2,1,0:T(8,128)(2,1)S(1)}, bf16[2,8,72,128]{3,2,1,0:T(8,128)(2,1)S(1)}, u32[]{:S(2)}, u32[]{:S(2)}) collective-permute-start(bf16[2,8,72,128]{3,2,1,0:T(8,128)(2,1)S(1)} %get-tuple-element.44), channel_id=1, source_target_pairs={{0,16},{1,2},{2,1},{3,19},{4,20},{5,6},{6,5},{7,23},{8,24},{9,10},... | collective-permute-start | bytes 884744 | tf_op jit(solution)/shard_map/ppermute | solution.py:58
  16.3 5.0 %copy-start = (bf16[2,64,256]{2,1,0:T(8,128)(2,1)S(1)}, bf16[2,64,256]{2,1,0:T(8,128)(2,1)}, u32[]{:S(2)}) copy-start(bf16[2,64,256]{2,1,0:T(8,128)(2,1)} %refs_8_.3) | copy-start | bytes 196612
  25.0 5.3 %collective-permute-start.8 = (bf16[7,64,128]{2,1,0:T(8,128)(2,1)S(1)}, bf16[7,64,128]{2,1,0:T(8,128)(2,1)S(1)}, u32[]{:S(2)}, u32[]{:S(2)}) collective-permute-start(bf16[7,64,128]{2,1,0:T(8,128)(2,1)S(1)} %get-tuple-element.54.refs_3_.block_ref.refs_7_), channel_id=1, source_target_pairs={{0,16},{1,2},{2,1},{3,19},{4,20},{5,6},{6,5},{7,23},{8,24},{9,10},... | collective-permute-start | bytes 344072 | tf_op jit(solution)/shard_map/ppermute | solution.py:58
  25.1 5.3 %collective-permute-start.7 = (bf16[7,64,128]{2,1,0:T(8,128)(2,1)S(1)}, bf16[7,64,128]{2,1,0:T(8,128)(2,1)S(1)}, u32[]{:S(2)}, u32[]{:S(2)}) collective-permute-start(bf16[7,64,128]{2,1,0:T(8,128)(2,1)S(1)} %get-tuple-element.54.refs_3_.block_ref.refs_7_), channel_id=1, source_target_pairs={{0,4},{4,0},{8,12},{12,8},{1,5},{5,1},{9,13},{13,9},{2,6},{6,2},{1... | collective-permute-start | bytes 344072 | tf_op jit(solution)/shard_map/ppermute | solution.py:45
  27.6 2.8 %collective-permute-start.6 = (bf16[7,64,128]{2,1,0:T(8,128)(2,1)S(1)}, bf16[7,64,128]{2,1,0:T(8,128)(2,1)S(1)}, u32[]{:S(2)}, u32[]{:S(2)}) collective-permute-start(bf16[7,64,128]{2,1,0:T(8,128)(2,1)S(1)} %get-tuple-element.54.refs_3_.block_ref.refs_7_), channel_id=1, source_target_pairs={{0,1},{1,0},{2,3},{3,2},{4,8},{5,9},{6,10},{7,11},{8,4},{9,5},{10,... | collective-permute-start | bytes 344072 | tf_op jit(solution)/shard_map/ppermute | solution.py:58
  30.5 2.7 %collective-permute-start.10 = (bf16[3,7,64,128]{3,2,1,0:T(8,128)(2,1)S(1)}, bf16[3,7,64,128]{3,2,1,0:T(8,128)(2,1)S(1)}, u32[]{:S(2)}, u32[]{:S(2)}) collective-permute-start(bf16[3,7,64,128]{3,2,1,0:T(8,128)(2,1)S(1)} %get-tuple-element.61), channel_id=1, source_target_pairs={{0,1},{1,0},{2,3},{3,2},{4,5},{5,4},{6,7},{7,6},{8,9},{9,8},{10,11... | collective-permute-start | bytes 1032200 | tf_op jit(solution)/shard_map/ppermute | solution.py:45
  31.9 5.7 %collective-permute-start.9 = (bf16[2,7,64,128]{3,2,1,0:T(8,128)(2,1)S(1)}, bf16[2,7,64,128]{3,2,1,0:T(8,128)(2,1)S(1)}, u32[]{:S(2)}, u32[]{:S(2)}) collective-permute-start(bf16[2,7,64,128]{3,2,1,0:T(8,128)(2,1)S(1)} %get-tuple-element.59), channel_id=1, source_target_pairs={{0,16},{1,2},{2,1},{3,19},{4,20},{5,6},{6,5},{7,23},{8,24},{9,10},... | collective-permute-start | bytes 688136 | tf_op jit(solution)/shard_map/ppermute | solution.py:58

commit v3 on v2

--- a/solution.py
+++ b/solution.py
@@ -269,10 +269,10 @@
         norm = centre_ref[row, 3] * scale
         items = [(c, dx) for c in range(len(feats)) for dx in range(3)]
         total = None
-        for k in range(0, len(items), 2):
+        for k in range(0, len(items), 6):
             weights = [[], []]
             vals = []
-            for c, dx in items[k : k + 2]:
+            for c, dx in items[k : k + 6]:
                 near = near_ref[c, row + dx] * scale
                 power = norm + near[3:4, :]
                 for d in range(3):

time: 41.8 us -> 41.6 us (level)
  no operation moved by 1% of the time
where the time goes in v3:
time: 41.6 us; the launch traced here: 41.1 us
  Pallas kernels  20.3 us (49%)
  starting transfers between devices  14.4 us (35%)
  waiting for transfers between devices  6.31 us (15%)
    pallas_call x6, Pallas kernels, gather_call(): pl.pallas_call(body, out_shape=tuple(outs), in_specs=[scalars(), scalars(...  18.5 us
    ppermute x4, starting transfers between devices, partner(): return lax.ppermute(block, axis, [(i, i ^ 1) for i in range(count)])  6.43 us
    ppermute x6, starting transfers between devices, whole_swap(): return lax.ppermute(block, axes, pairs)  5.81 us
    ppermute x4, waiting for transfers between devices, partner(): return lax.ppermute(block, axis, [(i, i ^ 1) for i in range(count)])  2.73 us
    ppermute x1, starting transfers between devices, local(): other = lax.ppermute(edge, 'gx', [(0, 1), (1, 0)])  2.12 us
    ppermute x6, waiting for transfers between devices, whole_swap(): return lax.ppermute(block, axes, pairs)  2.03 us
    ppermute x1, waiting for transfers between devices, local(): other = lax.ppermute(edge, 'gx', [(0, 1), (1, 0)])  1.55 us
    pallas_call x1, Pallas kernels, pack(): pl.pallas_call(body, out_shape=(jax.ShapeDtypeStruct((rows, width + HEAD,...  0.97 us
  transfers between devices with their start and end apart: 11, of which 6 were waited for; matrix products, arithmetic and copies ran while one was open for 0% of the time, Pallas kernels for 27%

profile of v3, /device:TPU:1, one launch (start us, length us, event | category | flops | bytes accessed | tf_op | source)
XLA Modules:
  0.0 41.1 jit_solution(4295241479949725037)
XLA Ops:
  0.0 1.0 %shard_map.109 = (bf16[6,72,128]{2,1,0:T(8,128)(2,1)S(1)}, bf16[3,72,128]{2,1,0:T(8,128)(2,1)S(1)}, s32[1,128]{1,0:T(1,128)S(1)}, f32[1,128]{1,0:T(1,128)S(1)}) custom-call(bf16[8,1,1,64,128]{4,3,2,1,0:T(8,128)(2,1)} %feat_ref.1, bf16[3,8,128]{2,1,0:T(8,128)(2,1)} %bitcast.10, s32[8]{0:T(128)} %bitcast.11, s32[3]{0:T(128)} %old_in.1, s32[3]{0:T(128)} %new_in.1, ...), custom_call_target="tpu_custom_call" | custom-call | tf_op jit(solution)/shard_map/pallas_call | solution.py:177
  1.0 2.1 %collective-permute-start = (bf16[3,72,128]{2,1,0:T(8,128)(2,1)S(1)}, bf16[3,72,128]{2,1,0:T(8,128)(2,1)S(1)}, u32[]{:S(2)}, u32[]{:S(2)}) collective-permute-start(bf16[3,72,128]{2,1,0:T(8,128)(2,1)S(1)} %get-tuple-element.40), channel_id=1, source_target_pairs={{0,16},{16,0},{1,17},{17,1},{2,18},{18,2},{3,19},{19,3},{4,20},{20... | collective-permute-start | bytes 165896 | tf_op jit(solution)/shard_map/ppermute | solution.py:537
  3.1 1.5 %collective-permute-done.other_ref = bf16[3,72,128]{2,1,0:T(8,128)(2,1)S(1)} collective-permute-done((bf16[3,72,128]{2,1,0:T(8,128)(2,1)S(1)}, bf16[3,72,128]{2,1,0:T(8,128)(2,1)S(1)}, u32[]{:S(2)}, u32[]{:S(2)}) %collective-permute-start) | collective-permute-done | bytes 55328 | tf_op jit(solution)/shard_map/ppermute | solution.py:537
  4.6 0.6 %shard_map.110.refs_2_.refs_3_.block_ref.refs_6_ = bf16[8,72,128]{2,1,0:T(8,128)(2,1)S(1)} custom-call(s32[1,128]{1,0:T(1,128)S(1)} %get-tuple-element.37.int_ref.refs_0_, bf16[6,72,128]{2,1,0:T(8,128)(2,1)S(1)} %get-tuple-element.39.mine_ref, bf16[3,72,128]{2,1,0:T(8,128)(2,1)S(1)} %collective-permute-done.other_ref), custom_call_target="tpu_custom_call" | custom-call | tf_op jit(solution)/shard_map/pallas_call | solution.py:216
  5.3 3.2 %collective-permute-start.3 = (bf16[8,72,128]{2,1,0:T(8,128)(2,1)S(1)}, bf16[8,72,128]{2,1,0:T(8,128)(2,1)S(1)}, u32[]{:S(2)}, u32[]{:S(2)}) collective-permute-start(bf16[8,72,128]{2,1,0:T(8,128)(2,1)S(1)} %shard_map.110.refs_2_.refs_3_.block_ref.refs_6_), channel_id=1, source_target_pairs={{0,16},{1,2},{2,1},{3,19},{4,20},{5,6},{6,5},{7,23},{8,24},{9,10},... | collective-permute-start | bytes 442376 | tf_op jit(solution)/shard_map/ppermute | solution.py:58
  8.5 1.3 %collective-permute-start.2 = (bf16[8,72,128]{2,1,0:T(8,128)(2,1)S(1)}, bf16[8,72,128]{2,1,0:T(8,128)(2,1)S(1)}, u32[]{:S(2)}, u32[]{:S(2)}) collective-permute-start(bf16[8,72,128]{2,1,0:T(8,128)(2,1)S(1)} %shard_map.110.refs_2_.refs_3_.block_ref.refs_6_), channel_id=1, source_target_pairs={{0,4},{4,0},{8,12},{12,8},{1,5},{5,1},{9,13},{13,9},{2,6},{6,2},{1... | collective-permute-start | bytes 442376 | tf_op jit(solution)/shard_map/ppermute | solution.py:45
  9.8 0.7 %collective-permute-start.1 = (bf16[8,72,128]{2,1,0:T(8,128)(2,1)S(1)}, bf16[8,72,128]{2,1,0:T(8,128)(2,1)S(1)}, u32[]{:S(2)}, u32[]{:S(2)}) collective-permute-start(bf16[8,72,128]{2,1,0:T(8,128)(2,1)S(1)} %shard_map.110.refs_2_.refs_3_.block_ref.refs_6_), channel_id=1, source_target_pairs={{0,1},{1,0},{2,3},{3,2},{4,8},{5,9},{6,10},{7,11},{8,4},{9,5},{10,... | collective-permute-start | bytes 442376 | tf_op jit(solution)/shard_map/ppermute | solution.py:58
  10.5 2.2 %shard_map.111 = (f32[7,64,256]{2,1,0:T(8,128)S(1)}, f32[8,4,128,128]{3,2,1,0:T(8,128)S(1)}, f32[1,10,8,128]{3,2,1,0:T(8,128)S(1)}, bf16[64,128]{1,0:T(8,128)(2,...) custom-call(s32[1,128]{1,0:T(1,128)S(1)} %get-tuple-element.37.int_ref.refs_0_, ...), custom_call_target="tpu_custom_call" | custom-call | flops 93585408 | bytes 1376256 | tf_op jit(solution)/shard_map/pallas_call | solution.py:500
  12.7 0.0 collective-permute-done.3.refs_6_
  12.7 0.7 %collective-permute-done.2.down_ref.refs_4_ = bf16[8,72,128]{2,1,0:T(8,128)(2,1)S(1)} collective-permute-done((bf16[8,72,128]{2,1,0:T(8,128)(2,1)S(1)}, bf16[8,72,128]{2,1,0:T(8,128)(2,1)S(1)}, u32[]{:S(2)}, u32[]{:S(2)}) %collective-permute-start.2) | collective-permute-done | bytes 147488 | tf_op jit(solution)/shard_map/ppermute | solution.py:45
  13.5 0.0 collective-permute-done.1.up_ref.refs_3_
  13.5 0.1 shard_map.112
  13.6 1.3 %collective-permute-start.5 = (bf16[3,8,72,128]{3,2,1,0:T(8,128)(2,1)S(1)}, bf16[3,8,72,128]{3,2,1,0:T(8,128)(2,1)S(1)}, u32[]{:S(2)}, u32[]{:S(2)}) collective-permute-start(bf16[3,8,72,128]{3,2,1,0:T(8,128)(2,1)S(1)} %get-tuple-element.46), channel_id=1, source_target_pairs={{0,1},{1,0},{2,3},{3,2},{4,5},{5,4},{6,7},{7,6},{8,9},{9,8},{10,11... | collective-permute-start | bytes 1327112 | tf_op jit(solution)/shard_map/ppermute | solution.py:45
  14.9 0.0 collective-permute-start.4
  14.9 1.4 %collective-permute-done.5.refs_5_ = bf16[3,8,72,128]{3,2,1,0:T(8,128)(2,1)S(1)} collective-permute-done((bf16[3,8,72,128]{3,2,1,0:T(8,128)(2,1)S(1)}, bf16[3,8,72,128]{3,2,1,0:T(8,128)(2,1)S(1)}, u32[]{:S(2)}, u32[]{:S(2)}) %collective-permute-start.5) | collective-permute-done | bytes 442400 | tf_op jit(solution)/shard_map/ppermute | solution.py:45
  16.3 0.0 copy-start
  16.3 4.0 %shard_map.113 = (f32[7,64,256]{2,1,0:T(8,128)S(1)}, f32[6,10,8,128]{3,2,1,0:T(8,128)S(1)}) custom-call(s32[1,128]{1,0:T(1,128)S(1)} %get-tuple-element.37.int_ref.refs_0_, f32[1,128]{1,0:T(1,128)S(1)} %get-tuple-element.38.refs_1_, bf16[8,72,128]{2,1,0:T(8,128)(2,1)S(1)} %shard_map.110.refs_2_.refs_3_.block_ref.refs_6_, ...), custom_call_target="tpu_custom_call" | custom-call | flops 561512448 | bytes 8257536 | tf_op jit(solution)/shard_map/pallas_call | solution.py:500
  20.3 1.0 %collective-permute-done.4.refs_3_ = bf16[2,8,72,128]{3,2,1,0:T(8,128)(2,1)S(1)} collective-permute-done((bf16[2,8,72,128]{3,2,1,0:T(8,128)(2,1)S(1)}, bf16[2,8,72,128]{3,2,1,0:T(8,128)(2,1)S(1)}, u32[]{:S(2)}, u32[]{:S(2)}) %collective-permute-start.4) | collective-permute-done | bytes 294944 | tf_op jit(solution)/shard_map/ppermute | solution.py:58
  21.3 0.0 copy-done
  21.3 3.4 %shard_map.114 = (bf16[7,64,128]{2,1,0:T(8,128)(2,1)S(1)}, f32[2,10,8,128]{3,2,1,0:T(8,128)S(1)}) custom-call(s32[1,128]{1,0:T(1,128)S(1)} %get-tuple-element.37.int_ref.refs_0_, f32[1,128]{1,0:T(1,128)S(1)} %get-tuple-element.38.refs_1_, bf16[8,72,128]{2,1,0:T(8,128)(2,1)S(1)} %shard_map.110.refs_2_.refs_3_.block_ref.refs_6_, ...), custom_call_target="tpu_custom_call" | custom-call | flops 187170816 | bytes 2752512 | tf_op jit(solution)/shard_map/pallas_call | solution.py:500
  24.7 0.1 collective-permute-start.8
  24.8 2.5 %collective-permute-start.7 = (bf16[7,64,128]{2,1,0:T(8,128)(2,1)S(1)}, bf16[7,64,128]{2,1,0:T(8,128)(2,1)S(1)}, u32[]{:S(2)}, u32[]{:S(2)}) collective-permute-start(bf16[7,64,128]{2,1,0:T(8,128)(2,1)S(1)} %get-tuple-element.54.refs_3_.block_ref.refs_7_), channel_id=1, source_target_pairs={{0,4},{4,0},{8,12},{12,8},{1,5},{5,1},{9,13},{13,9},{2,6},{6,2},{1... | collective-permute-start | bytes 344072 | tf_op jit(solution)/shard_map/ppermute | solution.py:45
  27.3 1.1 %collective-permute-start.6 = (bf16[7,64,128]{2,1,0:T(8,128)(2,1)S(1)}, bf16[7,64,128]{2,1,0:T(8,128)(2,1)S(1)}, u32[]{:S(2)}, u32[]{:S(2)}) collective-permute-start(bf16[7,64,128]{2,1,0:T(8,128)(2,1)S(1)} %get-tuple-element.54.refs_3_.block_ref.refs_7_), channel_id=1, source_target_pairs={{0,1},{1,0},{2,3},{3,2},{4,8},{5,9},{6,10},{7,11},{8,4},{9,5},{10,... | collective-permute-start | bytes 344072 | tf_op jit(solution)/shard_map/ppermute | solution.py:58
  28.4 1.7 %shard_map.115 = (f32[8,64,256]{2,1,0:T(8,128)S(1)}, bf16[64,128]{1,0:T(8,128)(2,1)S(1)}, bf16[256,64]{1,0:T(8,128)(2,1)S(1)}, f32[256,256]{1,0:T(8,128)S(1)}, f32[64,256]{1,0:T(8,128)S(1)}) custom-call(s32[1,128]{1,0:T(1,128)S(1)} %get-tuple-element.37.int_ref.refs_0_, f32[1,128]{1,0:T(1,128)S(1)} %get-tuple-element.38.refs_1_, ...), custom_call_target="tpu_custom_call" | custom-call | flops 106954752 | bytes 1572864 | tf_op jit(solution)/shard_map/pallas_call | solution.py:500
  30.1 0.0 collective-permute-done.8.refs_6_
  30.1 0.0 collective-permute-done.7.down_ref.refs_4_
  30.2 0.0 collective-permute-done.6.up_ref.refs_3_
  30.2 0.1 shard_map.116
  30.2 1.3 %collective-permute-start.10 = (bf16[3,7,64,128]{3,2,1,0:T(8,128)(2,1)S(1)}, bf16[3,7,64,128]{3,2,1,0:T(8,128)(2,1)S(1)}, u32[]{:S(2)}, u32[]{:S(2)}) collective-permute-start(bf16[3,7,64,128]{3,2,1,0:T(8,128)(2,1)S(1)} %get-tuple-element.61), channel_id=1, source_target_pairs={{0,1},{1,0},{2,3},{3,2},{4,5},{5,4},{6,7},{7,6},{8,9},{9,8},{10,11... | collective-permute-start | bytes 1032200 | tf_op jit(solution)/shard_map/ppermute | solution.py:45
  31.5 0.7 %collective-permute-start.9 = (bf16[2,7,64,128]{3,2,1,0:T(8,128)(2,1)S(1)}, bf16[2,7,64,128]{3,2,1,0:T(8,128)(2,1)S(1)}, u32[]{:S(2)}, u32[]{:S(2)}) collective-permute-start(bf16[2,7,64,128]{3,2,1,0:T(8,128)(2,1)S(1)} %get-tuple-element.59), channel_id=1, source_target_pairs={{0,16},{1,2},{2,1},{3,19},{4,20},{5,6},{6,5},{7,23},{8,24},{9,10},... | collective-permute-start | bytes 688136 | tf_op jit(solution)/shard_map/ppermute | solution.py:58
  32.2 0.6 %collective-permute-done.10.refs_5_ = bf16[3,7,64,128]{3,2,1,0:T(8,128)(2,1)S(1)} collective-permute-done((bf16[3,7,64,128]{3,2,1,0:T(8,128)(2,1)S(1)}, bf16[3,7,64,128]{3,2,1,0:T(8,128)(2,1)S(1)}, u32[]{:S(2)}, u32[]{:S(2)}) %collective-permute-start.10) | collective-permute-done | bytes 344096 | tf_op jit(solution)/shard_map/ppermute | solution.py:45
  32.8 3.4 %shard_map.117.refs_6_ = f32[8,64,256]{2,1,0:T(8,128)S(1)} custom-call(s32[1,128]{1,0:T(1,128)S(1)} %get-tuple-element.37.int_ref.refs_0_, f32[1,128]{1,0:T(1,128)S(1)} %get-tuple-element.38.refs_1_, bf16[8,72,128]{2,1,0:T(8,128)(2,1)S(1)} %shard_map.110.refs_2_.refs_3_.block_ref.refs_6_, bf16[7,64,128]{2,1,0:T(8,128)(2,1)S(1)} %collective-permute-done.6.up_ref.refs_3_, ...), custom_call_target="tpu_custom_call" | custom-call | flops 641728512 | bytes 9437184 | tf_op jit(solution)/shard_map/pallas_call | solution.py:500
  36.2 1.0 %collective-permute-done.9.refs_3_ = bf16[2,7,64,128]{3,2,1,0:T(8,128)(2,1)S(1)} collective-permute-done((bf16[2,7,64,128]{3,2,1,0:T(8,128)(2,1)S(1)}, bf16[2,7,64,128]{3,2,1,0:T(8,128)(2,1)S(1)}, u32[]{:S(2)}, u32[]{:S(2)}) %collective-permute-start.9) | collective-permute-done | bytes 229408 | tf_op jit(solution)/shard_map/ppermute | solution.py:58
  37.3 3.8 %shard_map.118 = bf16[8,64,128]{2,1,0:T(8,128)(2,1)} custom-call(s32[1,128]{1,0:T(1,128)S(1)} %get-tuple-element.37.int_ref.refs_0_, f32[1,128]{1,0:T(1,128)S(1)} %get-tuple-element.38.refs_1_, bf16[8,72,128]{2,1,0:T(8,128)(2,1)S(1)} %shard_map.110.refs_2_.refs_3_.block_ref.refs_6_, bf16[2,7,64,128]{3,2,1,0:T(8,128)(2,1)S(1)} %collective-permute-done.9.refs_3_, ...), custom_call_target="tpu_custom_call" | custom-call | flops 213909504 | bytes 3145728 | tf_op jit(solution)/shard_map/pallas_call | solution.py:500
Async XLA Ops:
  1.0 3.7 %collective-permute-start = (bf16[3,72,128]{2,1,0:T(8,128)(2,1)S(1)}, bf16[3,72,128]{2,1,0:T(8,128)(2,1)S(1)}, u32[]{:S(2)}, u32[]{:S(2)}) collective-permute-start(bf16[3,72,128]{2,1,0:T(8,128)(2,1)S(1)} %get-tuple-element.40), channel_id=1, source_target_pairs={{0,16},{16,0},{1,17},{17,1},{2,18},{18,2},{3,19},{19,3},{4,20},{20... | collective-permute-start | bytes 165896 | tf_op jit(solution)/shard_map/ppermute | solution.py:537
  5.3 7.5 %collective-permute-start.3 = (bf16[8,72,128]{2,1,0:T(8,128)(2,1)S(1)}, bf16[8,72,128]{2,1,0:T(8,128)(2,1)S(1)}, u32[]{:S(2)}, u32[]{:S(2)}) collective-permute-start(bf16[8,72,128]{2,1,0:T(8,128)(2,1)S(1)} %shard_map.110.refs_2_.refs_3_.block_ref.refs_6_), channel_id=1, source_target_pairs={{0,16},{1,2},{2,1},{3,19},{4,20},{5,6},{6,5},{7,23},{8,24},{9,10},... | collective-permute-start | bytes 442376 | tf_op jit(solution)/shard_map/ppermute | solution.py:58
  8.5 5.0 %collective-permute-start.2 = (bf16[8,72,128]{2,1,0:T(8,128)(2,1)S(1)}, bf16[8,72,128]{2,1,0:T(8,128)(2,1)S(1)}, u32[]{:S(2)}, u32[]{:S(2)}) collective-permute-start(bf16[8,72,128]{2,1,0:T(8,128)(2,1)S(1)} %shard_map.110.refs_2_.refs_3_.block_ref.refs_6_), channel_id=1, source_target_pairs={{0,4},{4,0},{8,12},{12,8},{1,5},{5,1},{9,13},{13,9},{2,6},{6,2},{1... | collective-permute-start | bytes 442376 | tf_op jit(solution)/shard_map/ppermute | solution.py:45
  9.8 3.7 %collective-permute-start.1 = (bf16[8,72,128]{2,1,0:T(8,128)(2,1)S(1)}, bf16[8,72,128]{2,1,0:T(8,128)(2,1)S(1)}, u32[]{:S(2)}, u32[]{:S(2)}) collective-permute-start(bf16[8,72,128]{2,1,0:T(8,128)(2,1)S(1)} %shard_map.110.refs_2_.refs_3_.block_ref.refs_6_), channel_id=1, source_target_pairs={{0,1},{1,0},{2,3},{3,2},{4,8},{5,9},{6,10},{7,11},{8,4},{9,5},{10,... | collective-permute-start | bytes 442376 | tf_op jit(solution)/shard_map/ppermute | solution.py:58
  13.6 2.8 %collective-permute-start.5 = (bf16[3,8,72,128]{3,2,1,0:T(8,128)(2,1)S(1)}, bf16[3,8,72,128]{3,2,1,0:T(8,128)(2,1)S(1)}, u32[]{:S(2)}, u32[]{:S(2)}) collective-permute-start(bf16[3,8,72,128]{3,2,1,0:T(8,128)(2,1)S(1)} %get-tuple-element.46), channel_id=1, source_target_pairs={{0,1},{1,0},{2,3},{3,2},{4,5},{5,4},{6,7},{7,6},{8,9},{9,8},{10,11... | collective-permute-start | bytes 1327112 | tf_op jit(solution)/shard_map/ppermute | solution.py:45
  14.9 6.4 %collective-permute-start.4 = (bf16[2,8,72,128]{3,2,1,0:T(8,128)(2,1)S(1)}, bf16[2,8,72,128]{3,2,1,0:T(8,128)(2,1)S(1)}, u32[]{:S(2)}, u32[]{:S(2)}) collective-permute-start(bf16[2,8,72,128]{3,2,1,0:T(8,128)(2,1)S(1)} %get-tuple-element.44), channel_id=1, source_target_pairs={{0,16},{1,2},{2,1},{3,19},{4,20},{5,6},{6,5},{7,23},{8,24},{9,10},... | collective-permute-start | bytes 884744 | tf_op jit(solution)/shard_map/ppermute | solution.py:58
  16.3 5.0 %copy-start = (bf16[2,64,256]{2,1,0:T(8,128)(2,1)S(1)}, bf16[2,64,256]{2,1,0:T(8,128)(2,1)}, u32[]{:S(2)}) copy-start(bf16[2,64,256]{2,1,0:T(8,128)(2,1)} %refs_8_.3) | copy-start | bytes 196612
  24.7 5.4 %collective-permute-start.8 = (bf16[7,64,128]{2,1,0:T(8,128)(2,1)S(1)}, bf16[7,64,128]{2,1,0:T(8,128)(2,1)S(1)}, u32[]{:S(2)}, u32[]{:S(2)}) collective-permute-start(bf16[7,64,128]{2,1,0:T(8,128)(2,1)S(1)} %get-tuple-element.54.refs_3_.block_ref.refs_7_), channel_id=1, source_target_pairs={{0,16},{1,2},{2,1},{3,19},{4,20},{5,6},{6,5},{7,23},{8,24},{9,10},... | collective-permute-start | bytes 344072 | tf_op jit(solution)/shard_map/ppermute | solution.py:58
  24.8 5.3 %collective-permute-start.7 = (bf16[7,64,128]{2,1,0:T(8,128)(2,1)S(1)}, bf16[7,64,128]{2,1,0:T(8,128)(2,1)S(1)}, u32[]{:S(2)}, u32[]{:S(2)}) collective-permute-start(bf16[7,64,128]{2,1,0:T(8,128)(2,1)S(1)} %get-tuple-element.54.refs_3_.block_ref.refs_7_), channel_id=1, source_target_pairs={{0,4},{4,0},{8,12},{12,8},{1,5},{5,1},{9,13},{13,9},{2,6},{6,2},{1... | collective-permute-start | bytes 344072 | tf_op jit(solution)/shard_map/ppermute | solution.py:45
  27.3 2.9 %collective-permute-start.6 = (bf16[7,64,128]{2,1,0:T(8,128)(2,1)S(1)}, bf16[7,64,128]{2,1,0:T(8,128)(2,1)S(1)}, u32[]{:S(2)}, u32[]{:S(2)}) collective-permute-start(bf16[7,64,128]{2,1,0:T(8,128)(2,1)S(1)} %get-tuple-element.54.refs_3_.block_ref.refs_7_), channel_id=1, source_target_pairs={{0,1},{1,0},{2,3},{3,2},{4,8},{5,9},{6,10},{7,11},{8,4},{9,5},{10,... | collective-permute-start | bytes 344072 | tf_op jit(solution)/shard_map/ppermute | solution.py:58
  30.2 2.6 %collective-permute-start.10 = (bf16[3,7,64,128]{3,2,1,0:T(8,128)(2,1)S(1)}, bf16[3,7,64,128]{3,2,1,0:T(8,128)(2,1)S(1)}, u32[]{:S(2)}, u32[]{:S(2)}) collective-permute-start(bf16[3,7,64,128]{3,2,1,0:T(8,128)(2,1)S(1)} %get-tuple-element.61), channel_id=1, source_target_pairs={{0,1},{1,0},{2,3},{3,2},{4,5},{5,4},{6,7},{7,6},{8,9},{9,8},{10,11... | collective-permute-start | bytes 1032200 | tf_op jit(solution)/shard_map/ppermute | solution.py:45
  31.5 5.7 %collective-permute-start.9 = (bf16[2,7,64,128]{3,2,1,0:T(8,128)(2,1)S(1)}, bf16[2,7,64,128]{3,2,1,0:T(8,128)(2,1)S(1)}, u32[]{:S(2)}, u32[]{:S(2)}) collective-permute-start(bf16[2,7,64,128]{3,2,1,0:T(8,128)(2,1)S(1)} %get-tuple-element.59), channel_id=1, source_target_pairs={{0,16},{1,2},{2,1},{3,19},{4,20},{5,6},{6,5},{7,23},{8,24},{9,10},... | collective-permute-start | bytes 688136 | tf_op jit(solution)/shard_map/ppermute | solution.py:58
